TPU v7x, 128 devices: a whole 4x4x4 slice. The times are simulated.
128 devices in a mesh: ctxa: 8 (over x, core), ctxb: 16 (over z, y).
Axes of the slice: x: 4, y: 4, z: 4, core: 2. Of those that a mesh axis runs over, the one named last changes fastest.
Arguments:
- tokens: bfloat16 [65536, 2048], P(('ctxa', 'ctxb')), may hold values from -6 to 6
- cotangent: bfloat16 [65536, 2048], P(('ctxa', 'ctxb')), may hold values from -6 to 6
- w_query: bfloat16 [2048, 1024], replicated, may hold values from -0.125 to 0.125
- w_key: bfloat16 [2048, 1024], replicated, may hold values from -0.125 to 0.125
- w_value: bfloat16 [2048, 1024], replicated, may hold values from -0.125 to 0.125
- w_out: bfloat16 [1024, 2048], replicated, may hold values from -0.125 to 0.125
Outputs:
- grad_tokens: bfloat16 [65536, 2048], P(('ctxa', 'ctxb'))
All inputs are finite; a program needn't handle non-finite values.
Results may differ from a plain program's by a relative error of at most 0.012.
Values may be sent and summed in bfloat16 or wider, within the bound.
A program may use at most 256 MiB of HBM per device.

v0:
```python
import math

import jax
import jax.numpy as jnp
from jax import lax
from jax.sharding import PartitionSpec as P

H = 8
DH = 128


def prefix(x, axis, join, neutral, backward):
    count = lax.axis_size(axis)
    place = lax.axis_index(axis)
    ahead = count - 1 - place if backward else place
    gathered = lax.all_gather(x.astype(jnp.bfloat16), axis)
    state = jnp.zeros_like(x) + jnp.asarray(neutral, x.dtype)

    def one(lap, state):
        source = count - 1 - lap if backward else lap
        return join(state, lax.dynamic_index_in_dim(gathered, source, 0, False).astype(x.dtype))

    return lax.fori_loop(0, ahead, one, state)


def project(left, weight):
    return jnp.dot(left, weight, preferred_element_type=jnp.float32).astype(jnp.bfloat16)


def add_states(earlier, later):
    return earlier + later


def regrouped_states(key_state, grad_state):
    key_group, grad_group = (
        lax.all_to_all(key_state[None], "ctxa", split_axis=1, concat_axis=0, tiled=True),
        lax.all_to_all(grad_state[None], "ctxa", split_axis=1, concat_axis=0, tiled=True),
    )
    key_total, grad_total = lax.psum((key_group, grad_group), "ctxb")
    key_row = prefix(key_group, "ctxb", add_states, jnp.zeros_like(key_group), False)
    grad_row = prefix(grad_group, "ctxb", add_states, jnp.zeros_like(grad_group), True)
    key_prior = jnp.cumsum(key_total, axis=0) - key_total + key_row
    grad_later = (
        jnp.sum(grad_total, axis=0, keepdims=True) - jnp.cumsum(grad_total, axis=0) + grad_row
    )
    key_prior = key_prior.astype(jnp.bfloat16)
    grad_later = grad_later.astype(jnp.bfloat16)
    returned = (
        lax.all_to_all(key_prior, "ctxa", split_axis=0, concat_axis=1, tiled=True),
        lax.all_to_all(grad_later, "ctxa", split_axis=0, concat_axis=1, tiled=True),
    )
    return (returned[0][0], returned[1][0])


def shards(tokens, cotangent, w_query, w_key, w_value, w_out):
    rows = tokens.shape[0]
    factor = 1.0 / math.sqrt(DH * rows * lax.axis_size("ctxa") * lax.axis_size("ctxb"))
    query = project(tokens, w_query).reshape(rows, H, DH)
    keys = project(tokens, w_key).reshape(rows, H, DH)
    values = project(tokens, w_value).reshape(rows, H, DH)
    grad_out = lax.dot_general(
        cotangent, w_out, (((1,), (1,)), ((), ())), preferred_element_type=jnp.float32
    )
    grad_out = grad_out.astype(jnp.bfloat16).reshape(rows, H, DH)
    key_state = jnp.einsum("rhi,rhj->hij", keys, values, preferred_element_type=jnp.float32)
    grad_state = jnp.einsum("rhi,rhj->hij", query, grad_out, preferred_element_type=jnp.float32)
    prior, later = regrouped_states(key_state, grad_state)
    index = jnp.arange(rows)
    causal = (index[:, None] >= index[None, :])[None]
    attend = jnp.where(
        causal, jnp.einsum("thi,shi->hts", query, keys, preferred_element_type=jnp.float32), 0.0
    ).astype(jnp.bfloat16)
    probe = jnp.where(
        causal,
        jnp.einsum("thj,shj->hts", grad_out, values, preferred_element_type=jnp.float32),
        0.0,
    ).astype(jnp.bfloat16)
    grad_query = jnp.einsum("hts,shi->thi", probe, keys, preferred_element_type=jnp.float32)
    grad_query = grad_query + jnp.einsum(
        "thj,hij->thi", grad_out, prior, preferred_element_type=jnp.float32
    )
    grad_key = jnp.einsum("hts,thi->shi", probe, query, preferred_element_type=jnp.float32)
    grad_key = grad_key + jnp.einsum(
        "shj,hij->shi", values, later, preferred_element_type=jnp.float32
    )
    grad_value = jnp.einsum("hts,thj->shj", attend, grad_out, preferred_element_type=jnp.float32)
    grad_value = grad_value + jnp.einsum(
        "shi,hij->shj", keys, later, preferred_element_type=jnp.float32
    )

    def finish(partial_grad):
        return (factor * partial_grad).astype(jnp.bfloat16).reshape(rows, H * DH)

    total = jnp.dot(finish(grad_query), w_query.T, preferred_element_type=jnp.float32)
    total = total + jnp.dot(finish(grad_key), w_key.T, preferred_element_type=jnp.float32)
    total = total + jnp.dot(finish(grad_value), w_value.T, preferred_element_type=jnp.float32)
    return total.astype(jnp.bfloat16)


def solution(mesh):
    placed = (P(("ctxa", "ctxb"), None), P(("ctxa", "ctxb"), None), P(), P(), P(), P())
    return jax.shard_map(
        shards, mesh=mesh, in_specs=placed, out_specs=P(("ctxa", "ctxb"), None), check_vma=False
    )
```

profile of v0, /device:TPU:0, one launch (start us, length us, event | category | flops | bytes accessed | tf_op | source)
XLA Modules:
  0.0 310.2 jit_solution(6295105417670766009)
XLA Ops:
  6.5 1.6 copy-done
  8.1 4.8 %fusion.5 = bf16[64,8,8,128]{3,2,1,0:T(8,128)(2,1)S(1)} fusion(bf16[512,2048]{1,0:T(8,128)(2,1)S(1)} %copy-done, bf16[2048,1024]{1,0:T(8,128)(2,1)} %param.13), kind=kOutput, calls=%fused_computation.16 | convolution fusion | flops 2148007936 | bytes 7340032 | tf_op jit(solution)/shard_map/dot_general | solution.py:27
  12.9 2.4 fusion.6
  16.3 1.4 convolution_bitcast_fusion.1
  17.7 4.4 %all-to-all-start = ((f32[1,8,128,128]{3,2,0,1:T(8,128)}), f32[1,8,128,128]{3,2,0,1:T(8,128)}, u32[]{:S(2)}, u32[]{:S(2)}) async-start(f32[1,8,128,128]{3,2,0,1:T(8,128)} %convolution_bitcast_fusion.1), calls=%async_computation | async-start | bytes 1048576 | tf_op jit(solution)/shard_map/all_to_all | solution.py:36
  22.1 5.6 %fusion.7 = bf16[64,8,8,128]{3,2,1,0:T(8,128)(2,1)} fusion(bf16[512,2048]{1,0:T(8,128)(2,1)S(1)} %copy-done, bf16[2048,1024]{1,0:T(8,128)(2,1)} %param.12), kind=kOutput, calls=%fused_computation.18 | convolution fusion | flops 2148007936 | bytes 7340032 | tf_op jit(solution)/shard_map/dot_general | solution.py:27
  27.8 3.3 %convolution_convert_fusion.2 = bf16[512,1024]{1,0:T(8,128)(2,1)} fusion(bf16[512,2048]{1,0:T(8,128)(2,1)S(1)} %copy-done.14, bf16[1024,2048]{1,0:T(8,128)(2,1)S(1)} %copy-done.9), kind=kOutput, calls=%fused_computation.14 | convolution fusion | flops 2148007936 | bytes 7340032 | tf_op jit(solution)/shard_map/dot_general | solution.py:61
  31.1 1.5 copy.49
  32.6 2.9 convolution_bitcast_fusion
  35.5 4.8 %all-to-all-start.2 = ((f32[1,8,128,128]{3,2,0,1:T(8,128)}), f32[1,8,128,128]{3,2,0,1:T(8,128)}, u32[]{:S(2)}, u32[]{:S(2)}) async-start(f32[1,8,128,128]{3,2,0,1:T(8,128)} %convolution_bitcast_fusion), calls=%async_computation.2 | async-start | bytes 1048576 | tf_op jit(solution)/shard_map/all_to_all | solution.py:37
  40.3 1.8 convert_bitcast_fusion.1
  42.1 8.6 %all-to-all-done.2 = f32[1,8,128,128]{3,2,0,1:T(8,128)} async-done(((f32[1,8,128,128]{3,2,0,1:T(8,128)}), f32[1,8,128,128]{3,2,0,1:T(8,128)}, u32[]{:S(2)}, u32[]{:S(2)}) %all-to-all-start.2) | async-done | bytes 524320 | tf_op jit(solution)/shard_map/all_to_all | solution.py:37
  50.7 1.8 convert_bitcast_fusion
  54.8 2.7 select_convert_fusion.1
  57.5 2.1 fusion.15
  59.7 2.9 fusion.25
  62.5 4.9 %fusion = f32[8,128,512]{2,1,0:T(8,128)} fusion(bf16[512,8,128]{0,2,1:T(8,128)(2,1)S(1)} %bitcast.111, pred[512,512]{1,0:T(8,128)(4,1)S(1)} %iota_compare_fusion, bf16[64,8,8,128]{3,2,1,0:T(8,128)(2,1)} %fusion.7, bf16[64,8,8,128]{3,2,1,0:T(8,128)(2,1)} %copy-done.2), kind=kOutput, calls=%fused_computation.4 | convolution fusion | flops 1077936128 | bytes 5505024 | tf_op jit(solution)/shard_map/hts,thj->shj/dot_general | solution.py:86
  67.4 77.3 %all-reduce.3.cloned.1.call-done = (f32[8,1,128,128]{3,2,0,1:T(8,128)}, f32[8,1,128,128]{3,2,0,1:T(8,128)}) async-done(((f32[8,1,128,128]{3,2,0,1:T(8,128)}, f32[8,1,128,128]{3,2,0,1:T(8,128)}), (f32[8,1,128,128]{3,2,0,1:T(8,128)}, f32[8,1,128,128]{3,2,0,1:T(8,128)})) %all-reduce.3.cloned.1.call-update) | async-done | bytes 1048592 | tf_op jit(solution)/shard_map/psum | solution.py:39
  145.8 52.0 %all-gather.5.cloned.1.call-done = bf16[16,8,128,128]{3,2,1,0:T(8,128)(2,1)} async-done(((bf16[1,8,128,128]{3,2,1,0:T(8,128)(2,1)}), bf16[16,8,128,128]{3,2,1,0:T(8,128)(2,1)}) %all-gather.5.cloned.1.call-update) | async-done | bytes 4194320 | tf_op jit(solution)/shard_map/all_gather | solution.py:16
  197.9 53.2 %all-gather.7.cloned.1.call-done = bf16[16,8,128,128]{3,2,1,0:T(8,128)(2,1)} async-done(((bf16[1,8,128,128]{3,2,1,0:T(8,128)(2,1)}), bf16[16,8,128,128]{3,2,1,0:T(8,128)(2,1)}) %all-gather.7.cloned.1.call-update) | async-done | bytes 4194320 | tf_op jit(solution)/shard_map/all_gather | solution.py:16
  251.1 16.4 %while.23 = (s32[]{:T(128)}, f32[8,1,128,128]{3,2,1,0:T(8,128)S(1)}, s32[]{:T(128)}, bf16[16,8,1,128,128]{4,3,1,2,0:T(8,128)(2,1)}, s32[]{:T(128)}, /*index=5*/s32[]{:T(128)}, s32[]{:T(128)}, s32[]{:T(128)}) while((s32[]{:T(128)}, f32[8,1,128,128]{3,2,1,0:T(8,128)S(1)}, s32[]{:T(128)}, bf16[16,8,1,128,128]{4,3,1,2,0:T(8,128)(2,1)}, s32[]{:T(128)}, ...), condition=%wide.region_8.9_spmd, body=%wide.region_7.8_spmd.sunk | while | flops 262150 | bytes 1310863 | solution.py:23
  267.5 2.0 fusion.11
  269.5 4.3 %all-to-all-start.1 = ((bf16[8,1,128,128]{3,2,1,0:T(8,128)(2,1)}), bf16[8,1,128,128]{3,2,1,0:T(8,128)(2,1)S(1)}, u32[]{:S(2)}, u32[]{:S(2)}) async-start(bf16[8,1,128,128]{3,2,1,0:T(8,128)(2,1)} %fusion.11), calls=%async_computation.1 | async-start | bytes 524288 | tf_op jit(solution)/shard_map/all_to_all | solution.py:49
  273.7 1.8 fusion.13
  275.5 5.7 %all-to-all-done.1 = bf16[8,1,128,128]{3,2,1,0:T(8,128)(2,1)S(1)} async-done(((bf16[8,1,128,128]{3,2,1,0:T(8,128)(2,1)}), bf16[8,1,128,128]{3,2,1,0:T(8,128)(2,1)S(1)}, u32[]{:S(2)}, u32[]{:S(2)}) %all-to-all-start.1) | async-done | bytes 262176 | tf_op jit(solution)/shard_map/all_to_all | solution.py:49
  281.2 3.6 %all-to-all-start.3 = ((bf16[8,1,128,128]{3,2,1,0:T(8,128)(2,1)}), bf16[8,1,128,128]{3,2,1,0:T(8,128)(2,1)S(1)}, u32[]{:S(2)}, u32[]{:S(2)}) async-start(bf16[8,1,128,128]{3,2,1,0:T(8,128)(2,1)} %fusion.13), calls=%async_computation.3 | async-start | bytes 524288 | tf_op jit(solution)/shard_map/all_to_all | solution.py:50
  284.9 2.5 multiply_convert_fusion.2
  288.0 4.3 %fusion.44 = f32[512,2048]{1,0:T(8,128)} fusion(bf16[512,1024]{0,1:T(8,128)(2,1)S(1)} %bitcast.114, bf16[2048,1024]{1,0:T(8,128)(2,1)S(1)} %copy-done.10), kind=kOutput, calls=%fused_computation.58 | convolution fusion | flops 2147483648 | bytes 9437184 | tf_op jit(solution)/shard_map/dot_general | solution.py:94
  292.3 2.2 multiply_convert_fusion.1
  295.2 2.4 fusion.45
  298.3 1.6 copy-done.13
  300.0 3.7 %add_convert_fusion = bf16[512,2048]{1,0:T(8,128)(2,1)} fusion(f32[512,2048]{1,0:T(8,128)S(1)} %copy-done.15, f32[512,2048]{1,0:T(8,128)S(1)} %fusion.45, bf16[512,1024]{0,1:T(8,128)(2,1)S(1)} %bitcast.113, bf16[2048,1024]{1,0:T(8,128)(2,1)S(1)} %copy-done.13), kind=kOutput, calls=%fused_computation.5 | convolution fusion | flops 2150629376 | bytes 15728640 | tf_op jit(solution)/shard_map/dot_general | solution.py:96
  (59 shorter events, 22.4 us)
Async XLA Ops:
  6.5 1.6 copy-start
  6.5 6.4 %copy-start.12 = (bf16[2048,1024]{1,0:T(8,128)(2,1)S(1)}, bf16[2048,1024]{1,0:T(8,128)(2,1)}, u32[]{:S(2)}) copy-start(bf16[2048,1024]{1,0:T(8,128)(2,1)} %param.14) | copy-start | bytes 12582916
  12.9 2.4 copy-start.2
  15.3 1.0 copy-start.7
  17.7 17.8 %all-to-all-start = ((f32[1,8,128,128]{3,2,0,1:T(8,128)}), f32[1,8,128,128]{3,2,0,1:T(8,128)}, u32[]{:S(2)}, u32[]{:S(2)}) async-start(f32[1,8,128,128]{3,2,0,1:T(8,128)} %convolution_bitcast_fusion.1), calls=%async_computation | async-start | bytes 1048576 | tf_op jit(solution)/shard_map/all_to_all | solution.py:36
  22.1 5.7 %copy-start.9 = (bf16[1024,2048]{1,0:T(8,128)(2,1)S(1)}, bf16[1024,2048]{1,0:T(8,128)(2,1)}, u32[]{:S(2)}) copy-start(bf16[1024,2048]{1,0:T(8,128)(2,1)} %param.15) | copy-start | bytes 12582916
  22.1 5.7 %copy-start.14 = (bf16[512,2048]{1,0:T(8,128)(2,1)S(1)}, bf16[512,2048]{1,0:T(8,128)(2,1)}, u32[]{:S(2)}) copy-start(bf16[512,2048]{1,0:T(8,128)(2,1)} %param.11) | copy-start | bytes 6291460
  32.6 30.0 %copy-start.1 = (bf16[512,1024]{0,1:T(8,128)(2,1)}, bf16[512,1024]{0,1:T(8,128)(2,1)S(1)}, u32[]{:S(2)}) copy-start(bf16[512,1024]{0,1:T(8,128)(2,1)S(1)} %copy.49) | copy-start | bytes 3145732
  35.5 15.2 %all-to-all-start.2 = ((f32[1,8,128,128]{3,2,0,1:T(8,128)}), f32[1,8,128,128]{3,2,0,1:T(8,128)}, u32[]{:S(2)}, u32[]{:S(2)}) async-start(f32[1,8,128,128]{3,2,0,1:T(8,128)} %convolution_bitcast_fusion), calls=%async_computation.2 | async-start | bytes 1048576 | tf_op jit(solution)/shard_map/all_to_all | solution.py:37
  52.5 92.2 %all-reduce.3.cloned.1.call-start = ((), (), s32[]{:S(2)}) async-start(), calls=%async_computation.6 | async-start | bytes 2097152 | tf_op jit(solution)/shard_map/psum | solution.py:39
  53.2 144.6 %all-gather.5.cloned.1.call-start = ((), (), s32[]{:S(2)}) async-start(), calls=%async_computation.4 | async-start | bytes 4456448 | tf_op jit(solution)/shard_map/all_gather | solution.py:16
  54.0 197.1 %all-gather.7.cloned.1.call-start = ((), (), s32[]{:S(2)}) async-start(), calls=%async_computation.5 | async-start | bytes 4456448 | tf_op jit(solution)/shard_map/all_gather | solution.py:16
  54.7 2.8 copy-start.5
  57.5 2.2 copy-start.3
  269.5 11.8 %all-to-all-start.1 = ((bf16[8,1,128,128]{3,2,1,0:T(8,128)(2,1)}), bf16[8,1,128,128]{3,2,1,0:T(8,128)(2,1)S(1)}, u32[]{:S(2)}, u32[]{:S(2)}) async-start(bf16[8,1,128,128]{3,2,1,0:T(8,128)(2,1)} %fusion.11), calls=%async_computation.1 | async-start | bytes 524288 | tf_op jit(solution)/shard_map/all_to_all | solution.py:49
  281.2 11.1 %all-to-all-start.3 = ((bf16[8,1,128,128]{3,2,1,0:T(8,128)(2,1)}), bf16[8,1,128,128]{3,2,1,0:T(8,128)(2,1)S(1)}, u32[]{:S(2)}, u32[]{:S(2)}) async-start(bf16[8,1,128,128]{3,2,1,0:T(8,128)(2,1)} %fusion.13), calls=%async_computation.3 | async-start | bytes 524288 | tf_op jit(solution)/shard_map/all_to_all | solution.py:50
  284.9 3.1 %copy-start.10 = (bf16[2048,1024]{1,0:T(8,128)(2,1)S(1)}, bf16[2048,1024]{1,0:T(8,128)(2,1)}, u32[]{:S(2)}) copy-start(bf16[2048,1024]{1,0:T(8,128)(2,1)} %param.12) | copy-start | bytes 12582916
  288.0 4.3 %copy-start.8 = (bf16[64,8,8,128]{3,2,1,0:T(8,128)(2,1)S(1)}, bf16[64,8,8,128]{3,2,1,0:T(8,128)(2,1)}, u32[]{:S(2)}) copy-start(bf16[64,8,8,128]{3,2,1,0:T(8,128)(2,1)} %copy-done.7) | copy-start | bytes 3145732
  292.3 2.8 copy-start.11
  295.2 2.4 copy-start.4
  295.2 2.4 copy-start.6
  295.2 3.2 %copy-start.15 = (f32[512,2048]{1,0:T(8,128)S(1)}, f32[512,2048]{1,0:T(8,128)}, u32[]{:S(2)}) copy-start(f32[512,2048]{1,0:T(8,128)} %fusion.44) | copy-start | bytes 12582916
  297.6 2.4 copy-start.13
Sparse Core Ops, SparseCore 0:
  56.6 88.0 all-reduce.2
  146.8 50.9 all-gather.4
  199.9 51.0 all-gather.6
where the time goes:
time: 313 us; the launch traced here: 310 us
  waiting for transfers between devices  199 us (64%)
  matrix products  48.6 us (16%)
  other arithmetic  24.5 us (8%)
  starting transfers between devices  17.3 us (6%)
  between operations  13.3 us (4%)
  local copies, waits for them, and re-layouts  7.27 us (2%)
    all_gather x2, waiting for transfers between devices, prefix(): gathered = lax.all_gather(x.astype(jnp.bfloat16), axis)  105 us
    psum x1, waiting for transfers between devices, regrouped_states(): key_total, grad_total = lax.psum((key_group, grad_group), 'ctxb')  77.3 us
    add x15, other arithmetic, add_states(): return earlier + later  16 us
    dot_general x3, matrix products, project(): jnp.dot(left, weight, preferred_element_type=jnp.float32)  12.8 us
    all_to_all x1, waiting for transfers between devices, regrouped_states(): lax.all_to_all(grad_state[None], 'ctxa', split_axis=1, concat_axis=0, til...  8.63 us
  transfers between devices with their start and end apart: 7, of which 5 were waited for; matrix products, arithmetic and copies ran while one was open for 12% of the time, Pallas kernels for 0%

commit v1 on v0

v1 whole, which is shorter than its diff:
```python
import functools
import math

import jax
import jax.numpy as jnp
from jax import lax
from jax.experimental import pallas as pl
from jax.experimental.pallas import tpu as pltpu
from jax.sharding import PartitionSpec as P

MESH = pl.DeviceIdType.MESH
F32 = jnp.float32
BF16 = jnp.bfloat16

DH = 128
PAIR = 2 * DH
PAIRS = 4
SUB = 256
NY = 4
NZ = 4
NA = 8
ROWS = DH // NY
CHUNK = 256


def dot(left, right, left_dim=1, right_dim=0):
    return lax.dot_general(
        left, right, (((left_dim,), (right_dim,)), ((), ())), preferred_element_type=F32
    )


def diagonal(first, second):
    zero = jnp.zeros_like(first)
    return jnp.concatenate(
        [jnp.concatenate([first, zero], axis=1), jnp.concatenate([zero, second], axis=1)], axis=0
    )


def kernel(
    factor,
    tok_h, cot_h, wq_h, wk_h, wv_h, wo_h, out_h,
    tok, cot, wall, wo, qkvg, intra, grads, acc, outs,
    local, sbuf, ybuf, zbuf, xbuf, back, pre,
    load_sem, out_sem,
    y_send, y_recv, z_send, z_recv, x_send, x_recv, b_send, b_recv,
):
    a = lax.axis_index("ctxa")
    b = lax.axis_index("ctxb")
    z, y = b // NY, b % NY

    def y_peer(step):
        return (a, z * NY + (y + step) % NY)

    def z_peer(step):
        return (a, ((z + step) % NZ) * NY + y)

    def x_peer(step):
        return ((a + step) % NA, b)

    barrier = pltpu.get_barrier_semaphore()
    peers = [y_peer(s) for s in range(1, NY)]
    peers += [z_peer(s) for s in range(1, NZ)]
    peers += [x_peer(s) for s in range(1, NA)]

    def columns(p, which):
        return pl.ds(pl.multiple_of((p % 2) * PAIR + which * 2 * PAIR, PAIR), PAIR)

    def weight_loads(p):
        cols = pl.ds(pl.multiple_of(p * PAIR, PAIR), PAIR)
        half = p // 2
        return [
            pltpu.make_async_copy(wk_h.at[:, cols], wall.at[half, :, columns(p, 1)], load_sem.at[p, 0]),
            pltpu.make_async_copy(wv_h.at[:, cols], wall.at[half, :, columns(p, 2)], load_sem.at[p, 1]),
            pltpu.make_async_copy(wq_h.at[:, cols], wall.at[half, :, columns(p, 0)], load_sem.at[p, 2]),
            pltpu.make_async_copy(wo_h.at[cols, :], wo.at[cols, :], load_sem.at[p, 3]),
        ]

    load_tok = pltpu.make_async_copy(tok_h, tok, load_sem.at[PAIRS, 0])
    load_cot = pltpu.make_async_copy(cot_h, cot, load_sem.at[PAIRS, 1])
    first = weight_loads(0)
    load_tok.start()
    first[0].start()
    first[1].start()
    first[2].start()
    load_cot.start()
    first[3].start()

    for peer in peers:
        pl.semaphore_signal(barrier, inc=1, device_id=peer, device_id_type=MESH)

    def y_copy(p, step):
        return pltpu.make_async_remote_copy(
            src_ref=sbuf.at[p, :, (y + step) % NY],
            dst_ref=ybuf.at[p, y],
            send_sem=y_send.at[p, step - 1],
            recv_sem=y_recv.at[p, step - 1],
            device_id=y_peer(step),
            device_id_type=MESH,
        )

    def z_copy(p, step):
        return pltpu.make_async_remote_copy(
            src_ref=zbuf.at[p, z],
            dst_ref=zbuf.at[p, z],
            send_sem=z_send.at[p, step - 1],
            recv_sem=z_recv.at[p, step - 1],
            device_id=z_peer(step),
            device_id_type=MESH,
        )

    def x_copy(p, step):
        return pltpu.make_async_remote_copy(
            src_ref=xbuf.at[p, a],
            dst_ref=xbuf.at[p, a],
            send_sem=x_send.at[p, step - 1],
            recv_sem=x_recv.at[p, step - 1],
            device_id=x_peer(step),
            device_id_type=MESH,
        )

    def b_copy(p, step):
        return pltpu.make_async_remote_copy(
            src_ref=back.at[p, (y + step) % NY],
            dst_ref=pre.at[p, :, y],
            send_sem=b_send.at[p, step - 1],
            recv_sem=b_recv.at[p, step - 1],
            device_id=y_peer(step),
            device_id_type=MESH,
        )

    def start_y(p):
        for step in range(1, NY):
            y_copy(p, step).start()

    def finish_y(p):
        ybuf[p, y] = sbuf[p, :, y]
        for step in range(1, NY):
            y_copy(p, step).wait_recv()
        total = ybuf[p, 0].astype(F32)
        for at in range(1, NY):
            total = total + ybuf[p, at].astype(F32)
        zbuf[p, z] = total.astype(BF16)

    def start_z(p):
        for step in range(1, NZ):
            z_copy(p, step).start()

    def finish_z(p):
        for step in range(1, NZ):
            z_copy(p, step).wait_recv()
        total = zbuf[p, 0].astype(F32)
        for at in range(1, NZ):
            total = total + zbuf[p, at].astype(F32)
        xbuf[p, a] = total.astype(BF16)

    def start_x(p):
        for step in range(1, NA):
            x_copy(p, step).start()

    def finish_x(p):
        for step in range(1, NA):
            x_copy(p, step).wait_recv()
        before = jnp.zeros((2, ROWS, DH), F32)
        after = jnp.zeros((2, ROWS, DH), F32)
        for at in range(NA):
            before = before + jnp.where(at < a, xbuf[p, at, 0:2].astype(F32), 0.0)
            after = after + jnp.where(at > a, xbuf[p, at, 2:4].astype(F32), 0.0)
        for at in range(NZ):
            before = before + jnp.where(at < z, zbuf[p, at, 0:2].astype(F32), 0.0)
            after = after + jnp.where(at > z, zbuf[p, at, 2:4].astype(F32), 0.0)
        for at in range(NY):
            back[p, at, 0:2] = before.astype(BF16)
            before = before + ybuf[p, at, 0:2].astype(F32)
        for at in reversed(range(NY)):
            back[p, at, 2:4] = after.astype(BF16)
            after = after + ybuf[p, at, 2:4].astype(F32)
        pre[p, :, y] = back[p, y]

    def start_b(p):
        for step in range(1, NY):
            b_copy(p, step).start()

    def finish_b(p):
        for step in range(1, NY):
            b_copy(p, step).wait_recv()

    load_tok.wait()

    def states(p, kind, left, right):
        for head in range(2):
            cols = slice(head * DH, (head + 1) * DH)
            parts = [
                dot(left[rows, cols], right[rows, cols], 0, 0)
                for rows in (slice(0, SUB), slice(SUB, 2 * SUB))
            ]
            local[p, 2 * kind + head] = parts[kind]
            total = (parts[0] + parts[1]).astype(BF16)
            sbuf[p, 2 * kind + head] = total.reshape(NY, ROWS, DH)

    def project(p, carry):
        half = p // 2

        @pl.when(p < PAIRS - 1)
        def _():
            for load in weight_loads(p + 1):
                load.start()

        loads = weight_loads(p)
        loads[0].wait()
        keys = dot(tok[...], wall[half, :, columns(p, 1)]).astype(BF16)
        qkvg[p, 1] = keys
        loads[1].wait()
        values = dot(tok[...], wall[half, :, columns(p, 2)]).astype(BF16)
        qkvg[p, 2] = values
        states(p, 0, keys, values)

        @pl.when(p >= 1)
        def _():
            finish_y(p - 1)

        @pl.when(p >= 2)
        def _():
            finish_z(p - 2)

        @pl.when(p >= 3)
        def _():
            finish_x(p - 3)

        loads[2].wait()
        query = dot(tok[...], wall[half, :, columns(p, 0)]).astype(BF16)
        qkvg[p, 0] = query

        @pl.when(p == 0)
        def _():
            pl.semaphore_wait(barrier, len(peers))

        @pl.when(p >= 1)
        def _():
            start_z(p - 1)

        @pl.when(p >= 2)
        def _():
            start_x(p - 2)

        @pl.when(p >= 3)
        def _():
            start_b(p - 3)

        loads[3].wait()

        @pl.when(p == 0)
        def _():
            load_cot.wait()

        rows = pl.ds(pl.multiple_of(p * PAIR, PAIR), PAIR)
        grad_out = dot(cot[...], wo[rows, :], 1, 1).astype(BF16)
        qkvg[p, 3] = grad_out
        states(p, 1, query, grad_out)

        start_y(p)
        return carry

    lax.fori_loop(0, PAIRS, project, 0)

    down = lax.broadcasted_iota(jnp.int32, (SUB, SUB), 0)
    across = lax.broadcasted_iota(jnp.int32, (SUB, SUB), 1)
    lower, upper = down >= across, across >= down

    def attention(p, carry):
        def one(n):
            head, block = n % 2, n // 2
            cols = slice(head * DH, (head + 1) * DH)
            rows = slice(block * SUB, (block + 1) * SUB)
            query, keys = qkvg[p, 0, rows, cols], qkvg[p, 1, rows, cols]
            values, grad_out = qkvg[p, 2, rows, cols], qkvg[p, 3, rows, cols]
            probe = jnp.where(lower, dot(grad_out, values, 1, 1), 0.0).astype(BF16)
            probe_t = jnp.where(upper, dot(values, grad_out, 1, 1), 0.0).astype(BF16)
            attend_t = jnp.where(upper, dot(keys, query, 1, 1), 0.0).astype(BF16)
            intra[p, 0, rows, cols] = dot(probe, keys)
            intra[p, 1, rows, cols] = dot(probe_t, query)
            intra[p, 2, rows, cols] = dot(attend_t, grad_out)

        one(0)
        one(1)

        @pl.when(p == 0)
        def _():
            finish_y(PAIRS - 1)

        @pl.when(p < 2)
        def _():
            finish_z(p + 2)

        @pl.when(p < 3)
        def _():
            finish_x(p + 1)

        one(2)

        @pl.when(p == 0)
        def _():
            start_z(PAIRS - 1)

        @pl.when(p < 2)
        def _():
            start_x(p + 2)

        @pl.when(p < 3)
        def _():
            start_b(p + 1)

        one(3)
        return carry

    lax.fori_loop(0, PAIRS, attention, 0)

    def between(p):
        finish_b(p)
        half = p // 2
        for block in range(2):
            rows = slice(block * SUB, (block + 1) * SUB)
            states_of = [pre[p, n].reshape(DH, DH) for n in range(4)]
            if block == 1:
                before = [(states_of[n].astype(F32) + local[p, n]).astype(BF16) for n in (0, 1)]
                after = states_of[2:]
            else:
                before = states_of[:2]
                after = [(states_of[n].astype(F32) + local[p, n]).astype(BF16) for n in (2, 3)]
            before, after = diagonal(*before), diagonal(*after)
            terms = [
                dot(qkvg[p, 3, rows], before, 1, 1),
                dot(qkvg[p, 2, rows], after, 1, 1),
                dot(qkvg[p, 1, rows], after, 1, 0),
            ]
            for which, term in enumerate(terms):
                grads[half, rows, columns(p, which)] = (
                    factor * (intra[p, which, rows] + term)
                ).astype(BF16)

    lax.fori_loop(0, 2, lambda p, c: (between(p), c)[1], 0)

    steps = wo.shape[1] // CHUNK

    def first_half(n, carry):
        rows = pl.ds(pl.multiple_of(n * CHUNK, CHUNK), CHUNK)
        acc[n] = dot(grads[0], wall[0, rows, :], 1, 1)
        return carry

    lax.fori_loop(0, steps, first_half, 0)
    lax.fori_loop(2, 4, lambda p, c: (between(p), c)[1], 0)

    def out_copy(n):
        cols = pl.ds(pl.multiple_of(n * CHUNK, CHUNK), CHUNK)
        return pltpu.make_async_copy(outs.at[n], out_h.at[:, cols], out_sem.at[n])

    def second_half(n, carry):
        rows = pl.ds(pl.multiple_of(n * CHUNK, CHUNK), CHUNK)
        outs[n] = (acc[n] + dot(grads[1], wall[1, rows, :], 1, 1)).astype(BF16)
        out_copy(n).start()
        return carry

    lax.fori_loop(0, steps, second_half, 0)

    def drain(p, carry):
        for step in range(1, NY):
            y_copy(p, step).wait_send()
            b_copy(p, step).wait_send()
        for step in range(1, NZ):
            z_copy(p, step).wait_send()
        for step in range(1, NA):
            x_copy(p, step).wait_send()
        return carry

    lax.fori_loop(0, PAIRS, drain, 0)
    lax.fori_loop(0, steps, lambda n, c: (out_copy(n).wait(), c)[1], 0)


def shards(tokens, cotangent, w_query, w_key, w_value, w_out):
    rows, width = tokens.shape
    blocks = lax.axis_size("ctxa") * lax.axis_size("ctxb")
    factor = 1.0 / math.sqrt(DH * rows * blocks)
    steps = width // CHUNK
    slot = (4, ROWS, DH)
    dma = pltpu.SemaphoreType.DMA
    return pl.pallas_call(
        functools.partial(kernel, factor),
        out_shape=jax.ShapeDtypeStruct((rows, width), BF16),
        in_specs=[pl.BlockSpec(memory_space=pl.ANY)] * 6,
        out_specs=pl.BlockSpec(memory_space=pl.ANY),
        scratch_shapes=[
            pltpu.VMEM((rows, width), BF16),
            pltpu.VMEM((rows, width), BF16),
            pltpu.VMEM((2, width, 6 * PAIR), BF16),
            pltpu.VMEM((PAIRS * PAIR, width), BF16),
            pltpu.VMEM((PAIRS, 4, rows, PAIR), BF16),
            pltpu.VMEM((PAIRS, 3, rows, PAIR), F32),
            pltpu.VMEM((2, rows, 6 * PAIR), BF16),
            pltpu.VMEM((steps, rows, CHUNK), F32),
            pltpu.VMEM((steps, rows, CHUNK), BF16),
            pltpu.VMEM((PAIRS, 4, DH, DH), F32),
            pltpu.VMEM((PAIRS, 4, NY, ROWS, DH), BF16),
            pltpu.VMEM((PAIRS, NY, *slot), BF16),
            pltpu.VMEM((PAIRS, NZ, *slot), BF16),
            pltpu.VMEM((PAIRS, NA, *slot), BF16),
            pltpu.VMEM((PAIRS, NY, *slot), BF16),
            pltpu.VMEM((PAIRS, 4, NY, ROWS, DH), BF16),
            dma((PAIRS + 1, 4)),
            dma((steps,)),
            dma((PAIRS, NY - 1)),
            dma((PAIRS, NY - 1)),
            dma((PAIRS, NZ - 1)),
            dma((PAIRS, NZ - 1)),
            dma((PAIRS, NA - 1)),
            dma((PAIRS, NA - 1)),
            dma((PAIRS, NY - 1)),
            dma((PAIRS, NY - 1)),
        ],
        compiler_params=pltpu.CompilerParams(
            collective_id=0, has_side_effects=True, vmem_limit_bytes=60 * 1024 * 1024
        ),
    )(tokens, cotangent, w_query, w_key, w_value, w_out)


def solution(mesh):
    placed = (P(("ctxa", "ctxb"), None), P(("ctxa", "ctxb"), None), P(), P(), P(), P())
    return jax.shard_map(
        shards, mesh=mesh, in_specs=placed, out_specs=P(("ctxa", "ctxb"), None), check_vma=False
    )
```

time: 313 us -> 66.6 us (0.21)
  waiting for transfers between devices: 199 us -> 0 us
  Pallas kernels: 0 us -> 62.2 us
  matrix products: 48.6 us -> 0 us
  other arithmetic: 24.5 us -> 0 us
  starting transfers between devices: 17.3 us -> 0 us
  between operations: 13.3 us -> 0.01 us
  local copies, waits for them, and re-layouts: 7.27 us -> 3.16 us
    all_gather x2 -> x0, waiting for transfers between devices: 105 us -> none  [prefix(): gathered = lax.all_gather(x.astype(jnp.bfloat16), axis)]
    psum x1 -> x0, waiting for transfers between devices: 77.3 us -> none  [regrouped_states(): key_total, grad_total = lax.psum((key_group, grad_group), 'ctxb')]
    pallas_call x0 -> x1, Pallas kernels: none -> 62.2 us  [shards(): pl.pallas_call(functools.partial(kernel, factor), out_shape=jax.ShapeDtyp...]
    dot_general x16 -> x0, matrix products: 48.6 us -> none  [the longest x3 12.8 us: project(): jnp.dot(left, weight, preferred_element_type=jnp.float32)]
    all_to_all x4 -> x0, starting transfers between devices: 17.1 us -> none  [the longest x1 4.79 us: regrouped_states(): lax.all_to_all(grad_state[None], 'ctxa', split_axis=1, concat_axis=0, til...]
    add x15 -> x0, other arithmetic: 16 us -> none  [add_states(): return earlier + later]
    all_to_all x4 -> x0, waiting for transfers between devices: 14.3 us -> none  [the longest x1 8.63 us: regrouped_states(): lax.all_to_all(grad_state[None], 'ctxa', split_axis=1, concat_axis=0, til...]
    another operation x2 -> x0, other arithmetic: 3.78 us -> none  [the longest x1 1.97 us: regrouped_states(): key_prior = jnp.cumsum(key_total, axis=0) - key_total + key_row]
  transfers between devices with their start and end apart: 7 -> 0, of which waited for: 5 -> 0; matrix products, arithmetic and copies ran while one was open for 12% -> 0% of each run, Pallas kernels for 0% -> 0%
where the time goes in v1:
time: 66.6 us; the launch traced here: 65.4 us
  Pallas kernels  62.2 us (93%)
  local copies, waits for them, and re-layouts  3.16 us (5%)
    pallas_call x1, Pallas kernels, shards(): pl.pallas_call(functools.partial(kernel, factor), out_shape=jax.ShapeDtyp...  62.2 us
    unnamed x1, local copies, waits for them, and re-layouts  3.16 us

profile of v1, /device:TPU:0, one launch (start us, length us, event | category | flops | bytes accessed | tf_op | source)
XLA Modules:
  0.0 65.4 jit_solution(3794413578677152930)
XLA Ops:
  0.0 62.2 %shard_map.64 = bf16[512,2048]{1,0:T(8,128)(2,1)} custom-call(bf16[512,2048]{1,0:T(8,128)(2,1)} %tok_h.1, bf16[512,2048]{1,0:T(8,128)(2,1)} %cot_h.1, bf16[2048,1024]{1,0:T(8,128)(2,1)} %wq_h.1, bf16[2048,1024]{1,0:T(8,128)(2,1)} %wk_h.1, bf16[2048,1024]{1,0:T(8,128)(2,1)} %wv_h.1, bf16[1024,2048]{1,0:T(8,128)(2,1)} %wo_h.1), custom_call_target="tpu_custom_call" | custom-call | tf_op jit(solution)/shard_map/pallas_call | solution.py:385
  62.3 3.2 %copy.8 = bf16[512,2048]{1,0:T(8,128)(2,1)} copy(bf16[512,2048]{1,0:T(8,128)(2,1)} %shard_map.64) | data formatting | bytes 4194304

commit v2 on v0

v2 whole, which is shorter than its diff:
```python
import functools
import math

import jax
import jax.numpy as jnp
from jax import lax
from jax.experimental import pallas as pl
from jax.experimental.pallas import tpu as pltpu
from jax.sharding import PartitionSpec as P

MESH = pl.DeviceIdType.MESH
F32 = jnp.float32
BF16 = jnp.bfloat16

DH = 128
PAIR = 2 * DH
PAIRS = 4
SUB = 256
NY = 4
NZ = 4
NA = 8
ROWS = DH // NY
CHUNK = 512
EARLY = 3 * 3 * PAIR


def dot(left, right, left_dim=1, right_dim=0):
    return lax.dot_general(
        left, right, (((left_dim,), (right_dim,)), ((), ())), preferred_element_type=F32
    )


def diagonal(first, second):
    zero = jnp.zeros_like(first)
    return jnp.concatenate(
        [jnp.concatenate([first, zero], axis=1), jnp.concatenate([zero, second], axis=1)], axis=0
    )


def kernel(
    factor,
    tok_h, cot_h, wq_h, wk_h, wv_h, wo_h, out,
    tok, cot, wall, wo, qkvg, intra, grads, acc,
    local, sbuf, ybuf, zbuf, xown, xbuf, back, pre,
    load_sem,
    y_send, y_recv, z_send, z_recv, x_send, x_recv, b_send, b_recv,
):
    a = lax.axis_index("ctxa")
    b = lax.axis_index("ctxb")
    z, y = b // NY, b % NY

    def y_peer(step):
        return (a, z * NY + (y + step) % NY)

    def z_peer(step):
        return (a, ((z + step) % NZ) * NY + y)

    def x_peer(step):
        return ((a + step) % NA, b)

    barrier = pltpu.get_barrier_semaphore()
    peers = [y_peer(s) for s in range(1, NY)]
    peers += [z_peer(s) for s in range(1, NZ)]
    peers += [x_peer(s) for s in range(1, NA)]

    def columns(p, which, count=1):
        return slice((3 * p + which) * PAIR, (3 * p + which + count) * PAIR)

    def weight(p, which):
        cols = slice(p * PAIR, (p + 1) * PAIR)
        if which == 3:
            return pltpu.make_async_copy(wo_h.at[cols, :], wo.at[cols, :], load_sem.at[4 * p + 3])
        source = (wq_h, wk_h, wv_h)[which]
        return pltpu.make_async_copy(
            source.at[:, cols], wall.at[:, columns(p, which)], load_sem.at[4 * p + which]
        )

    load_tok = pltpu.make_async_copy(tok_h, tok, load_sem.at[4 * PAIRS])
    load_cot = pltpu.make_async_copy(cot_h, cot, load_sem.at[4 * PAIRS + 1])
    loads = [
        [load_tok, weight(0, 1), weight(0, 2)],
        [weight(1, 1), weight(1, 2)],
        [load_cot, weight(0, 0), weight(0, 3)],
        [weight(1, 0), weight(1, 3)],
        [weight(2, 1), weight(2, 2)],
        [weight(3, 1), weight(3, 2)],
        [weight(2, 0), weight(2, 3)],
        [weight(3, 0), weight(3, 3)],
    ]

    def fetch(*groups):
        for group in groups:
            for load in loads[group]:
                load.start()

    def arrive(group):
        for load in loads[group]:
            load.wait()

    def remote(source, target, sent, received, device):
        return pltpu.make_async_remote_copy(
            src_ref=source, dst_ref=target, send_sem=sent, recv_sem=received,
            device_id=device, device_id_type=MESH,
        )

    def y_copy(p, step):
        return remote(
            sbuf.at[p, :, (y + step) % NY], ybuf.at[p, y],
            y_send.at[p, step - 1], y_recv.at[p, step - 1], y_peer(step),
        )

    def z_copy(p, step):
        return remote(
            zbuf.at[p, z], zbuf.at[p, z],
            z_send.at[p, step - 1], z_recv.at[p, step - 1], z_peer(step),
        )

    def x_copy(p, step):
        return remote(
            xown.at[p, (a + step) // NA], xbuf.at[p, a],
            x_send.at[p, step - 1], x_recv.at[p, step - 1], x_peer(step),
        )

    def b_copy(p, step):
        return remote(
            back.at[p, (y + step) % NY], pre.at[p, :, y],
            b_send.at[p, step - 1], b_recv.at[p, step - 1], y_peer(step),
        )

    def start(copy, count, p):
        for step in range(1, count):
            copy(p, step).start()

    def receive(copy, count, p):
        for step in range(1, count):
            copy(p, step).wait_recv()

    def finish_y(p):
        receive(y_copy, NY, p)
        ybuf[p, y] = sbuf[p, :, y]
        total = ybuf[p, 0].astype(F32)
        for at in range(1, NY):
            total = total + ybuf[p, at].astype(F32)
        zbuf[p, z] = total.astype(BF16)

    def finish_z(p):
        receive(z_copy, NZ, p)
        total = zbuf[p, 0].astype(F32)
        for at in range(1, NZ):
            total = total + zbuf[p, at].astype(F32)
        total = total.astype(BF16)
        xown[p, 0] = total[0:2]
        xown[p, 1] = total[2:4]

    def finish_x(p):
        receive(x_copy, NA, p)
        before = jnp.zeros((2, ROWS, DH), F32)
        after = jnp.zeros((2, ROWS, DH), F32)
        for at in range(NA):
            part = xbuf[p, at].astype(F32)
            before = before + jnp.where(at < a, part, 0.0)
            after = after + jnp.where(at > a, part, 0.0)
        for at in range(NZ):
            before = before + jnp.where(at < z, zbuf[p, at, 0:2].astype(F32), 0.0)
            after = after + jnp.where(at > z, zbuf[p, at, 2:4].astype(F32), 0.0)
        for at in range(NY):
            back[p, at, 0:2] = before.astype(BF16)
            before = before + ybuf[p, at, 0:2].astype(F32)
        for at in reversed(range(NY)):
            back[p, at, 2:4] = after.astype(BF16)
            after = after + ybuf[p, at, 2:4].astype(F32)
        pre[p, :, y] = back[p, y]

    def start_y(p):
        start(y_copy, NY, p)

    def start_z(p):
        start(z_copy, NZ, p)

    def start_x(p):
        start(x_copy, NA, p)

    def start_b(p):
        start(b_copy, NY, p)

    def states(p, kind, left, right):
        for head in range(2):
            cols = slice(head * DH, (head + 1) * DH)
            parts = [
                dot(left[rows, cols], right[rows, cols], 0, 0)
                for rows in (slice(0, SUB), slice(SUB, 2 * SUB))
            ]
            local[p, 2 * kind + head] = parts[kind]
            total = (parts[0] + parts[1]).astype(BF16)
            sbuf[p, 2 * kind + head] = total.reshape(NY, ROWS, DH)

    def keys_values(p):
        both = dot(tok[...], wall[:, columns(p, 1, 2)]).astype(BF16)
        keys, values = both[:, :PAIR], both[:, PAIR:]
        qkvg[p, 1] = keys
        qkvg[p, 2] = values
        states(p, 0, keys, values)

    def query_grad(p):
        query = dot(tok[...], wall[:, columns(p, 0)]).astype(BF16)
        grad_out = dot(cot[...], wo[p * PAIR : (p + 1) * PAIR], 1, 1).astype(BF16)
        qkvg[p, 0] = query
        qkvg[p, 3] = grad_out
        states(p, 1, query, grad_out)

    down = lax.broadcasted_iota(jnp.int32, (SUB, SUB), 0)
    across = lax.broadcasted_iota(jnp.int32, (SUB, SUB), 1)
    lower, upper = down >= across, across >= down

    def attention(p):
        for block in range(2):
            for head in range(2):
                cols = slice(head * DH, (head + 1) * DH)
                rows = slice(block * SUB, (block + 1) * SUB)
                query, keys = qkvg[p, 0, rows, cols], qkvg[p, 1, rows, cols]
                values, grad_out = qkvg[p, 2, rows, cols], qkvg[p, 3, rows, cols]
                probe = jnp.where(lower, dot(grad_out, values, 1, 1), 0.0).astype(BF16)
                probe_t = jnp.where(upper, dot(values, grad_out, 1, 1), 0.0).astype(BF16)
                attend_t = jnp.where(upper, dot(keys, query, 1, 1), 0.0).astype(BF16)
                intra[p, 0, rows, cols] = dot(probe, keys)
                intra[p, 1, rows, cols] = dot(probe_t, query)
                intra[p, 2, rows, cols] = dot(attend_t, grad_out)

    def between(p):
        states_of = [pre[p, n].reshape(DH, DH) for n in range(4)]
        for block in range(2):
            rows = slice(block * SUB, (block + 1) * SUB)
            own = (0, 1) if block == 1 else (2, 3)
            moved = [
                (states_of[n].astype(F32) + local[p, n]).astype(BF16) if n in own else states_of[n]
                for n in range(4)
            ]
            before, after = diagonal(*moved[:2]), diagonal(*moved[2:])
            terms = [
                dot(qkvg[p, 3, rows], before, 1, 1),
                dot(qkvg[p, 2, rows], after, 1, 1),
                dot(qkvg[p, 1, rows], after, 1, 0),
            ]
            for which, term in enumerate(terms):
                grads[rows, columns(p, which)] = (
                    factor * (intra[p, which, rows] + term)
                ).astype(BF16)

    def early(n):
        acc[n] = dot(grads[:, :EARLY], wall[n * CHUNK : (n + 1) * CHUNK, :EARLY], 1, 1)

    def late(n):
        part = dot(grads[:, EARLY:], wall[n * CHUNK : (n + 1) * CHUNK, EARLY:], 1, 1)
        out[:, n * CHUNK : (n + 1) * CHUNK] = (acc[n] + part).astype(BF16)

    fetch(0)
    for peer in peers:
        pl.semaphore_signal(barrier, inc=1, device_id=peer, device_id_type=MESH)
    arrive(0)
    fetch(1, 2)
    keys_values(0)

    arrive(1)
    fetch(3)
    keys_values(1)

    arrive(2)
    fetch(4)
    query_grad(0)

    arrive(3)
    fetch(5, 6, 7)
    pl.semaphore_wait(barrier, len(peers))
    start_y(0)
    query_grad(1)

    arrive(4)
    start_y(1)
    keys_values(2)

    arrive(5)
    finish_y(0)
    start_z(0)
    keys_values(3)

    arrive(6)
    finish_y(1)
    start_z(1)
    query_grad(2)

    arrive(7)
    finish_z(0)
    start_x(0)
    start_y(2)
    query_grad(3)

    finish_z(1)
    start_x(1)
    start_y(3)
    attention(0)

    finish_y(2)
    finish_x(0)
    start_z(2)
    start_b(0)
    attention(1)

    finish_y(3)
    finish_x(1)
    start_z(3)
    start_b(1)
    attention(2)

    finish_z(2)
    start_x(2)
    attention(3)

    finish_z(3)
    receive(b_copy, NY, 0)
    start_x(3)
    between(0)
    receive(b_copy, NY, 1)
    between(1)

    finish_x(2)
    start_b(2)
    receive(b_copy, NY, 2)
    between(2)
    finish_x(3)
    start_b(3)

    for n in range(4):
        early(n)
    receive(b_copy, NY, 3)
    between(3)
    for n in range(4):
        late(n)

    for p in range(PAIRS):
        for copy, count in ((y_copy, NY), (z_copy, NZ), (x_copy, NA), (b_copy, NY)):
            for step in range(1, count):
                copy(p, step).wait_send()


def shards(tokens, cotangent, w_query, w_key, w_value, w_out):
    rows, width = tokens.shape
    blocks = lax.axis_size("ctxa") * lax.axis_size("ctxb")
    factor = 1.0 / math.sqrt(DH * rows * blocks)
    slot = (4, ROWS, DH)
    half = (2, ROWS, DH)
    dma = pltpu.SemaphoreType.DMA
    return pl.pallas_call(
        functools.partial(kernel, factor),
        out_shape=pltpu.VMEM((rows, width), BF16),
        in_specs=[pl.BlockSpec(memory_space=pl.ANY)] * 6,
        out_specs=pl.BlockSpec(memory_space=pltpu.VMEM),
        scratch_shapes=[
            pltpu.VMEM((rows, width), BF16),
            pltpu.VMEM((rows, width), BF16),
            pltpu.VMEM((width, 3 * PAIRS * PAIR), BF16),
            pltpu.VMEM((PAIRS * PAIR, width), BF16),
            pltpu.VMEM((PAIRS, 4, rows, PAIR), BF16),
            pltpu.VMEM((PAIRS, 3, rows, PAIR), F32),
            pltpu.VMEM((rows, 3 * PAIRS * PAIR), BF16),
            pltpu.VMEM((width // CHUNK, rows, CHUNK), F32),
            pltpu.VMEM((PAIRS, 4, DH, DH), F32),
            pltpu.VMEM((PAIRS, 4, NY, ROWS, DH), BF16),
            pltpu.VMEM((PAIRS, NY, *slot), BF16),
            pltpu.VMEM((PAIRS, NZ, *slot), BF16),
            pltpu.VMEM((PAIRS, 2, *half), BF16),
            pltpu.VMEM((PAIRS, NA, *half), BF16),
            pltpu.VMEM((PAIRS, NY, *slot), BF16),
            pltpu.VMEM((PAIRS, 4, NY, ROWS, DH), BF16),
            dma((4 * PAIRS + 2,)),
            dma((PAIRS, NY - 1)),
            dma((PAIRS, NY - 1)),
            dma((PAIRS, NZ - 1)),
            dma((PAIRS, NZ - 1)),
            dma((PAIRS, NA - 1)),
            dma((PAIRS, NA - 1)),
            dma((PAIRS, NY - 1)),
            dma((PAIRS, NY - 1)),
        ],
        compiler_params=pltpu.CompilerParams(
            collective_id=0, has_side_effects=True, vmem_limit_bytes=56 * 1024 * 1024
        ),
    )(tokens, cotangent, w_query, w_key, w_value, w_out)


def solution(mesh):
    placed = (P(("ctxa", "ctxb"), None), P(("ctxa", "ctxb"), None), P(), P(), P(), P())
    return jax.shard_map(
        shards, mesh=mesh, in_specs=placed, out_specs=P(("ctxa", "ctxb"), None), check_vma=False
    )
```

time: 313 us -> 47.5 us (0.15)
  waiting for transfers between devices: 199 us -> 0 us
  matrix products: 48.6 us -> 0 us
  Pallas kernels: 0 us -> 46 us
  other arithmetic: 24.5 us -> 0 us
  starting transfers between devices: 17.3 us -> 0 us
  between operations: 13.3 us -> 0.01 us
  local copies, waits for them, and re-layouts: 7.27 us -> 1.32 us
    all_gather x2 -> x0, waiting for transfers between devices: 105 us -> none  [prefix(): gathered = lax.all_gather(x.astype(jnp.bfloat16), axis)]
    psum x1 -> x0, waiting for transfers between devices: 77.3 us -> none  [regrouped_states(): key_total, grad_total = lax.psum((key_group, grad_group), 'ctxb')]
    dot_general x16 -> x0, matrix products: 48.6 us -> none  [the longest x3 12.8 us: project(): jnp.dot(left, weight, preferred_element_type=jnp.float32)]
    pallas_call x0 -> x1, Pallas kernels: none -> 46 us  [shards(): pl.pallas_call(functools.partial(kernel, factor), out_shape=pltpu.VMEM((r...]
    all_to_all x4 -> x0, starting transfers between devices: 17.1 us -> none  [the longest x1 4.79 us: regrouped_states(): lax.all_to_all(grad_state[None], 'ctxa', split_axis=1, concat_axis=0, til...]
    add x15 -> x0, other arithmetic: 16 us -> none  [add_states(): return earlier + later]
    all_to_all x4 -> x0, waiting for transfers between devices: 14.3 us -> none  [the longest x1 8.63 us: regrouped_states(): lax.all_to_all(grad_state[None], 'ctxa', split_axis=1, concat_axis=0, til...]
    unnamed x32 -> x1, local copies, waits for them, and re-layouts: 5.71 us -> 1.32 us
  transfers between devices with their start and end apart: 7 -> 0, of which waited for: 5 -> 0; matrix products, arithmetic and copies ran while one was open for 12% -> 0% of each run, Pallas kernels for 0% -> 0%
where the time goes in v2:
time: 47.5 us; the launch traced here: 47.3 us
  Pallas kernels  46 us (97%)
  local copies, waits for them, and re-layouts  1.32 us (3%)
    pallas_call x1, Pallas kernels, shards(): pl.pallas_call(functools.partial(kernel, factor), out_shape=pltpu.VMEM((r...  46 us
    unnamed x1, local copies, waits for them, and re-layouts  1.32 us

profile of v2, /device:TPU:0, one launch (start us, length us, event | category | flops | bytes accessed | tf_op | source)
XLA Modules:
  0.0 47.3 jit_solution(11087295729120575453)
XLA Ops:
  0.0 46.0 %shard_map.64 = bf16[512,2048]{1,0:T(8,128)(2,1)S(1)} custom-call(bf16[512,2048]{1,0:T(8,128)(2,1)} %tok_h.1, bf16[512,2048]{1,0:T(8,128)(2,1)} %cot_h.1, bf16[2048,1024]{1,0:T(8,128)(2,1)} %wq_h.1, bf16[2048,1024]{1,0:T(8,128)(2,1)} %wk_h.1, bf16[2048,1024]{1,0:T(8,128)(2,1)} %wv_h.1, bf16[1024,2048]{1,0:T(8,128)(2,1)} %wo_h.1), custom_call_target="tpu_custom_call" | custom-call | tf_op jit(solution)/shard_map/pallas_call | solution.py:352
  46.0 1.3 %copy.8 = bf16[512,2048]{1,0:T(8,128)(2,1)} copy(bf16[512,2048]{1,0:T(8,128)(2,1)S(1)} %shard_map.64) | data formatting | bytes 4194304

commit v3 on v2

v3 whole, which is shorter than its diff:
```python
import functools
import math

import jax
import jax.numpy as jnp
from jax import lax
from jax.experimental import pallas as pl
from jax.experimental.pallas import tpu as pltpu
from jax.sharding import PartitionSpec as P

MESH = pl.DeviceIdType.MESH
F32 = jnp.float32
BF16 = jnp.bfloat16

DH = 128
PAIR = 2 * DH
PAIRS = 4
SUB = 256
NY = 4
NZ = 4
NA = 8
ROWS = DH // NY
CHUNK = 512
KEYS, GRADS = 0, PAIRS


K, G = KEYS, GRADS
ORDER = (
    ("got", 1), ("get", 3), ("ys", K), ("kv", 1),
    ("got", 2), ("get", 4), ("ys", K + 1), ("kv", 2),
    ("got", 3), ("get", 5), ("ys", K + 2), ("kv", 3),
    ("got", 4), ("get", 6), ("ys", K + 3), ("yf", K), ("zs", K), ("qg", 0),
    ("got", 5), ("get", 7), ("ys", G), ("yf", K + 1), ("zs", K + 1), ("qg", 1),
    ("got", 6), ("ys", G + 1), ("yf", K + 2), ("zs", K + 2), ("qg", 2),
    ("got", 7), ("ys", G + 2), ("yf", K + 3), ("zf", K), ("zs", K + 3), ("xs", K), ("qg", 3),
    ("ys", G + 3), ("yf", G), ("zf", K + 1), ("zs", G), ("xs", K + 1), ("a", 0),
    ("yf", G + 1), ("zf", K + 2), ("zs", G + 1), ("xs", K + 2), ("a", 1),
    ("yf", G + 2), ("zf", K + 3), ("xf", K), ("zs", G + 2), ("xs", K + 3), ("bs", K), ("a", 2),
    ("yf", G + 3), ("zf", G), ("xf", K + 1), ("zs", G + 3), ("xs", G), ("bs", K + 1), ("a", 3),
    ("zf", G + 1), ("xf", K + 2), ("xs", G + 1), ("bs", K + 2), ("bf", K), ("bq", 0), ("pq", 0),
    ("zf", G + 2), ("xf", K + 3), ("xs", G + 2), ("bs", K + 3), ("bf", K + 1), ("bq", 1), ("pq", 1),
    ("zf", G + 3), ("xf", G), ("xs", G + 3), ("bs", G), ("bf", K + 2), ("bq", 2), ("pq", 2),
    ("xf", G + 1), ("bs", G + 1), ("bf", K + 3), ("bq", 3), ("pq", 3),
    ("xf", G + 2), ("bs", G + 2), ("bf", G), ("br", 0), ("pr", 0),
    ("xf", G + 3), ("bs", G + 3), ("bf", G + 1), ("br", 1), ("pr", 1),
    ("bf", G + 2), ("br", 2), ("pr", 2),
    ("bf", G + 3), ("br", 3), ("pr", 3),
)


def dot(left, right, left_dim=1, right_dim=0):
    return lax.dot_general(
        left, right, (((left_dim,), (right_dim,)), ((), ())), preferred_element_type=F32
    )


def diagonal(first, second):
    zero = jnp.zeros_like(first)
    return jnp.concatenate(
        [jnp.concatenate([first, zero], axis=1), jnp.concatenate([zero, second], axis=1)], axis=0
    )


def kernel(
    factor,
    tok_h, cot_h, wq_h, wk_h, wv_h, wo_h, out,
    tok, cot, wall, wo, qkvg, intra, grads, acc,
    local, sbuf, ybuf, zbuf, xown, xbuf, back, pre,
    load_sem,
    y_send, y_recv, z_send, z_recv, x_send, x_recv, b_send, b_recv,
):
    a = lax.axis_index("ctxa")
    b = lax.axis_index("ctxb")
    z, y = b // NY, b % NY

    def y_peer(step):
        return (a, z * NY + (y + step) % NY)

    def z_peer(step):
        return (a, ((z + step) % NZ) * NY + y)

    def x_peer(step):
        return ((a + step) % NA, b)

    barrier = pltpu.get_barrier_semaphore()
    peers = [y_peer(s) for s in range(1, NY)]
    peers += [z_peer(s) for s in range(1, NZ)]
    peers += [x_peer(s) for s in range(1, NA)]

    def columns(p, which, count=1):
        first = p if which == 0 else PAIRS + 2 * p + which - 1
        return slice(first * PAIR, (first + count) * PAIR)

    def weight(p, which):
        cols = slice(p * PAIR, (p + 1) * PAIR)
        if which == 3:
            return pltpu.make_async_copy(wo_h.at[cols, :], wo.at[cols, :], load_sem.at[4 * p + 3])
        source = (wq_h, wk_h, wv_h)[which]
        return pltpu.make_async_copy(
            source.at[:, cols], wall.at[:, columns(p, which)], load_sem.at[4 * p + which]
        )

    load_tok = pltpu.make_async_copy(tok_h, tok, load_sem.at[4 * PAIRS])
    load_cot = pltpu.make_async_copy(cot_h, cot, load_sem.at[4 * PAIRS + 1])
    loads = [[load_tok, weight(0, 1), weight(0, 2)]]
    loads += [[weight(p, 1), weight(p, 2)] for p in range(1, PAIRS)]
    loads += [[load_cot, weight(0, 0), weight(0, 3)]]
    loads += [[weight(p, 0), weight(p, 3)] for p in range(1, PAIRS)]

    def fetch(group):
        for load in loads[group]:
            load.start()

    def arrive(group):
        for load in loads[group]:
            load.wait()

    def remote(source, target, sent, received, device):
        return pltpu.make_async_remote_copy(
            src_ref=source, dst_ref=target, send_sem=sent, recv_sem=received,
            device_id=device, device_id_type=MESH,
        )

    def y_copy(m, step):
        return remote(
            sbuf.at[m, :, (y + step) % NY], ybuf.at[m, y],
            y_send.at[m, step - 1], y_recv.at[m, step - 1], y_peer(step),
        )

    def z_copy(m, step):
        return remote(
            zbuf.at[m, z], zbuf.at[m, z],
            z_send.at[m, step - 1], z_recv.at[m, step - 1], z_peer(step),
        )

    def x_copy(m, step):
        return remote(
            xown.at[m], xbuf.at[m, a],
            x_send.at[m, step - 1], x_recv.at[m, step - 1], x_peer(step if m < GRADS else NA - step),
        )

    def b_copy(m, step):
        return remote(
            back.at[m, (y + step) % NY], pre.at[m, :, y],
            b_send.at[m, step - 1], b_recv.at[m, step - 1], y_peer(step),
        )

    def start(copy, count, m):
        for step in range(1, count):
            copy(m, step).start()

    def receive(copy, count, m):
        for step in range(1, count):
            copy(m, step).wait_recv()

    def x_each(m, sending, act):
        upward = (m < GRADS) == sending
        for step in range(1, NA):
            pl.when(a + step < NA if upward else a >= step)(functools.partial(act, m, step))

    def start_y(m):
        start(y_copy, NY, m)

    def start_z(m):
        start(z_copy, NZ, m)

    def start_x(m):
        x_each(m, True, lambda m, step: x_copy(m, step).start())

    def start_b(m):
        start(b_copy, NY, m)

    def finish_y(m):
        receive(y_copy, NY, m)
        ybuf[m, y] = sbuf[m, :, y]
        total = ybuf[m, 0].astype(F32)
        for at in range(1, NY):
            total = total + ybuf[m, at].astype(F32)
        zbuf[m, z] = total.astype(BF16)

    def finish_z(m):
        receive(z_copy, NZ, m)
        total = zbuf[m, 0].astype(F32)
        for at in range(1, NZ):
            total = total + zbuf[m, at].astype(F32)
        xown[m] = total.astype(BF16)

    def finish_x(m):
        x_each(m, False, lambda m, step: x_copy(m, step).wait_recv())
        keys = m < GRADS
        total = jnp.zeros((2, ROWS, DH), F32)
        for at in range(NA):
            total = total + jnp.where(at < a if keys else at > a, xbuf[m, at].astype(F32), 0.0)
        for at in range(NZ):
            total = total + jnp.where(at < z if keys else at > z, zbuf[m, at].astype(F32), 0.0)
        for at in range(NY) if keys else reversed(range(NY)):
            back[m, at] = total.astype(BF16)
            total = total + ybuf[m, at].astype(F32)
        pre[m, :, y] = back[m, y]

    def finish_b(m):
        receive(b_copy, NY, m)

    def states(p, kind, left, right):
        for head in range(2):
            cols = slice(head * DH, (head + 1) * DH)
            parts = [
                dot(left[rows, cols], right[rows, cols], 0, 0)
                for rows in (slice(0, SUB), slice(SUB, 2 * SUB))
            ]
            m = kind * PAIRS + p
            local[m, head] = parts[kind]
            sbuf[m, head] = (parts[0] + parts[1]).astype(BF16).reshape(NY, ROWS, DH)

    def keys_values(p):
        both = dot(tok[...], wall[:, columns(p, 1, 2)]).astype(BF16)
        keys, values = both[:, :PAIR], both[:, PAIR:]
        qkvg[p, 1] = keys
        qkvg[p, 2] = values
        states(p, 0, keys, values)

    def query_grad(p):
        query = dot(tok[...], wall[:, columns(p, 0)]).astype(BF16)
        grad_out = dot(cot[...], wo[p * PAIR : (p + 1) * PAIR], 1, 1).astype(BF16)
        qkvg[p, 0] = query
        qkvg[p, 3] = grad_out
        states(p, 1, query, grad_out)

    down = lax.broadcasted_iota(jnp.int32, (SUB, SUB), 0)
    across = lax.broadcasted_iota(jnp.int32, (SUB, SUB), 1)
    lower, upper = down >= across, across >= down

    def attention(p):
        for block in range(2):
            for head in range(2):
                cols = slice(head * DH, (head + 1) * DH)
                rows = slice(block * SUB, (block + 1) * SUB)
                query, keys = qkvg[p, 0, rows, cols], qkvg[p, 1, rows, cols]
                values, grad_out = qkvg[p, 2, rows, cols], qkvg[p, 3, rows, cols]
                probe = jnp.where(lower, dot(grad_out, values, 1, 1), 0.0).astype(BF16)
                probe_t = jnp.where(upper, dot(values, grad_out, 1, 1), 0.0).astype(BF16)
                attend_t = jnp.where(upper, dot(keys, query, 1, 1), 0.0).astype(BF16)
                intra[p, 0, rows, cols] = dot(probe, keys)
                intra[p, 1, rows, cols] = dot(probe_t, query)
                intra[p, 2, rows, cols] = dot(attend_t, grad_out)

    def moved(m, block):
        whole = [pre[m, head].reshape(DH, DH) for head in range(2)]
        if block == (1 if m < GRADS else 0):
            whole = [(whole[head].astype(F32) + local[m, head]).astype(BF16) for head in range(2)]
        return diagonal(*whole)

    def finish(p, which, rows, term):
        grads[rows, columns(p, which)] = (factor * (intra[p, which, rows] + term)).astype(BF16)

    def between_query(p):
        for block in range(2):
            rows = slice(block * SUB, (block + 1) * SUB)
            finish(p, 0, rows, dot(qkvg[p, 3, rows], moved(KEYS + p, block), 1, 1))

    def between_rest(p):
        for block in range(2):
            rows = slice(block * SUB, (block + 1) * SUB)
            after = moved(GRADS + p, block)
            finish(p, 1, rows, dot(qkvg[p, 2, rows], after, 1, 1))
            finish(p, 2, rows, dot(qkvg[p, 1, rows], after, 1, 0))

    def product(cols, first=False, last=False):
        for n in range(acc.shape[0]):
            rows = slice(n * CHUNK, (n + 1) * CHUNK)
            part = dot(grads[:, cols], wall[rows, cols], 1, 1)
            part = part if first else acc[n] + part
            if last:
                out[:, rows] = part.astype(BF16)
            else:
                acc[n] = part

    blocks = {
        "kv": keys_values, "qg": query_grad, "a": attention, "bq": between_query, "br": between_rest,
        "yf": finish_y, "zf": finish_z, "xf": finish_x, "bf": finish_b,
        "ys": start_y, "zs": start_z, "xs": start_x, "bs": start_b,
        "get": fetch, "got": arrive,
        "pq": lambda p: product(columns(p, 0), first=p == 0),
        "pr": lambda p: product(columns(p, 1, 2), last=p == PAIRS - 1),
    }

    fetch(0)
    for peer in peers:
        pl.semaphore_signal(barrier, inc=1, device_id=peer, device_id_type=MESH)
    arrive(0)
    fetch(1)
    fetch(2)
    keys_values(0)
    pl.semaphore_wait(barrier, len(peers))
    for name, at in ORDER:
        blocks[name](at)

    for m in range(2 * PAIRS):
        for copy, count in ((y_copy, NY), (z_copy, NZ), (b_copy, NY)):
            for step in range(1, count):
                copy(m, step).wait_send()
        x_each(m, True, lambda m, step: x_copy(m, step).wait_send())


def shards(tokens, cotangent, w_query, w_key, w_value, w_out):
    rows, width = tokens.shape
    blocks = lax.axis_size("ctxa") * lax.axis_size("ctxb")
    factor = 1.0 / math.sqrt(DH * rows * blocks)
    slot = (2, ROWS, DH)
    messages = 2 * PAIRS
    dma = pltpu.SemaphoreType.DMA
    return pl.pallas_call(
        functools.partial(kernel, factor),
        out_shape=pltpu.VMEM((rows, width), BF16),
        in_specs=[pl.BlockSpec(memory_space=pl.ANY)] * 6,
        out_specs=pl.BlockSpec(memory_space=pltpu.VMEM),
        scratch_shapes=[
            pltpu.VMEM((rows, width), BF16),
            pltpu.VMEM((rows, width), BF16),
            pltpu.VMEM((width, 3 * PAIRS * PAIR), BF16),
            pltpu.VMEM((PAIRS * PAIR, width), BF16),
            pltpu.VMEM((PAIRS, 4, rows, PAIR), BF16),
            pltpu.VMEM((PAIRS, 3, rows, PAIR), F32),
            pltpu.VMEM((rows, 3 * PAIRS * PAIR), BF16),
            pltpu.VMEM((width // CHUNK, rows, CHUNK), F32),
            pltpu.VMEM((messages, 2, DH, DH), F32),
            pltpu.VMEM((messages, 2, NY, ROWS, DH), BF16),
            pltpu.VMEM((messages, NY, *slot), BF16),
            pltpu.VMEM((messages, NZ, *slot), BF16),
            pltpu.VMEM((messages, *slot), BF16),
            pltpu.VMEM((messages, NA, *slot), BF16),
            pltpu.VMEM((messages, NY, *slot), BF16),
            pltpu.VMEM((messages, 2, NY, ROWS, DH), BF16),
            dma((4 * PAIRS + 2,)),
            dma((messages, NY - 1)),
            dma((messages, NY - 1)),
            dma((messages, NZ - 1)),
            dma((messages, NZ - 1)),
            dma((messages, NA - 1)),
            dma((messages, NA - 1)),
            dma((messages, NY - 1)),
            dma((messages, NY - 1)),
        ],
        compiler_params=pltpu.CompilerParams(
            collective_id=0, has_side_effects=True, vmem_limit_bytes=56 * 1024 * 1024
        ),
    )(tokens, cotangent, w_query, w_key, w_value, w_out)


def solution(mesh):
    placed = (P(("ctxa", "ctxb"), None), P(("ctxa", "ctxb"), None), P(), P(), P(), P())
    return jax.shard_map(
        shards, mesh=mesh, in_specs=placed, out_specs=P(("ctxa", "ctxb"), None), check_vma=False
    )
```

time: 47.5 us -> 42.3 us (0.89)
  Pallas kernels: 46 us -> 40.8 us
    pallas_call x1, Pallas kernels: 46 us -> 40.8 us  [shards(): pl.pallas_call(functools.partial(kernel, factor), out_shape=pltpu.VMEM((r...]
where the time goes in v3:
time: 42.3 us; the launch traced here: 42.2 us
  Pallas kernels  40.8 us (96%)
  local copies, waits for them, and re-layouts  1.32 us (3%)
    pallas_call x1, Pallas kernels, shards(): pl.pallas_call(functools.partial(kernel, factor), out_shape=pltpu.VMEM((r...  40.8 us
    unnamed x1, local copies, waits for them, and re-layouts  1.32 us

profile of v3, /device:TPU:0, one launch (start us, length us, event | category | flops | bytes accessed | tf_op | source)
XLA Modules:
  0.0 42.2 jit_solution(14068754862692573745)
XLA Ops:
  0.0 40.8 %shard_map.64 = bf16[512,2048]{1,0:T(8,128)(2,1)S(1)} custom-call(bf16[512,2048]{1,0:T(8,128)(2,1)} %tok_h.1, bf16[512,2048]{1,0:T(8,128)(2,1)} %cot_h.1, bf16[2048,1024]{1,0:T(8,128)(2,1)} %wq_h.1, bf16[2048,1024]{1,0:T(8,128)(2,1)} %wk_h.1, bf16[2048,1024]{1,0:T(8,128)(2,1)} %wv_h.1, bf16[1024,2048]{1,0:T(8,128)(2,1)} %wo_h.1), custom_call_target="tpu_custom_call" | custom-call | tf_op jit(solution)/shard_map/pallas_call | solution.py:312
  40.8 1.3 %copy.8 = bf16[512,2048]{1,0:T(8,128)(2,1)} copy(bf16[512,2048]{1,0:T(8,128)(2,1)S(1)} %shard_map.64) | data formatting | bytes 4194304

commit v4 on v3

--- a/solution.py
+++ b/solution.py
@@ -16,33 +16,35 @@
 PAIR = 2 * DH
 PAIRS = 4
 SUB = 256
+PARTS = 4
 NY = 4
 NZ = 4
 NA = 8
 ROWS = DH // NY
+DEPTH = 512
 CHUNK = 512
 KEYS, GRADS = 0, PAIRS
 
 
 K, G = KEYS, GRADS
 ORDER = (
-    ("got", 1), ("get", 3), ("ys", K), ("kv", 1),
-    ("got", 2), ("get", 4), ("ys", K + 1), ("kv", 2),
-    ("got", 3), ("get", 5), ("ys", K + 2), ("kv", 3),
-    ("got", 4), ("get", 6), ("ys", K + 3), ("yf", K), ("zs", K), ("qg", 0),
-    ("got", 5), ("get", 7), ("ys", G), ("yf", K + 1), ("zs", K + 1), ("qg", 1),
-    ("got", 6), ("ys", G + 1), ("yf", K + 2), ("zs", K + 2), ("qg", 2),
-    ("got", 7), ("ys", G + 2), ("yf", K + 3), ("zf", K), ("zs", K + 3), ("xs", K), ("qg", 3),
-    ("ys", G + 3), ("yf", G), ("zf", K + 1), ("zs", G), ("xs", K + 1), ("a", 0),
-    ("yf", G + 1), ("zf", K + 2), ("zs", G + 1), ("xs", K + 2), ("a", 1),
-    ("yf", G + 2), ("zf", K + 3), ("xf", K), ("zs", G + 2), ("xs", K + 3), ("bs", K), ("a", 2),
-    ("yf", G + 3), ("zf", G), ("xf", K + 1), ("zs", G + 3), ("xs", G), ("bs", K + 1), ("a", 3),
-    ("zf", G + 1), ("xf", K + 2), ("xs", G + 1), ("bs", K + 2), ("bf", K), ("bq", 0), ("pq", 0),
-    ("zf", G + 2), ("xf", K + 3), ("xs", G + 2), ("bs", K + 3), ("bf", K + 1), ("bq", 1), ("pq", 1),
-    ("zf", G + 3), ("xf", G), ("xs", G + 3), ("bs", G), ("bf", K + 2), ("bq", 2), ("pq", 2),
+    ("got", 4), ("kv", 1), ("ks", 0),
+    ("got", 5), ("get", 8), ("ys", K), ("kv", 2), ("ks", 1),
+    ("got", 6), ("get", 9), ("ys", K + 1), ("kv", 3), ("ks", 2),
+    ("got", 7), ("get", 10), ("ys", K + 2), ("qg", 0), ("ks", 3),
+    ("got", 8), ("ys", K + 3), ("yf", K), ("zs", K), ("qg", 1), ("gs", 0),
+    ("got", 9), ("ys", G), ("yf", K + 1), ("zs", K + 1), ("qg", 2), ("gs", 1),
+    ("got", 10), ("ys", G + 1), ("yf", K + 2), ("zs", K + 2), ("zf", K), ("xs", K), ("qg", 3), ("gs", 2), ("gs", 3),
+    ("ys", G + 2), ("ys", G + 3), ("yf", K + 3), ("zs", K + 3), ("zf", K + 1), ("xs", K + 1), ("yf", G), ("zs", G), ("a", 0),
+    ("zf", K + 2), ("xs", K + 2), ("yf", G + 1), ("zs", G + 1), ("a", 1),
+    ("xf", K), ("bs", K), ("zf", K + 3), ("xs", K + 3), ("a", 2),
+    ("xf", K + 1), ("bs", K + 1), ("yf", G + 2), ("zs", G + 2), ("yf", G + 3), ("zs", G + 3), ("zf", G), ("xs", G), ("a", 3),
+    ("zf", G + 1), ("xs", G + 1), ("xf", K + 2), ("bs", K + 2), ("bf", K), ("bq", 0), ("pq", 0),
+    ("xf", K + 3), ("bs", K + 3), ("zf", G + 2), ("xs", G + 2), ("bf", K + 1), ("bq", 1), ("pq", 1),
+    ("zf", G + 3), ("xs", G + 3), ("xf", G), ("bs", G), ("bf", K + 2), ("bq", 2), ("pq", 2),
     ("xf", G + 1), ("bs", G + 1), ("bf", K + 3), ("bq", 3), ("pq", 3),
-    ("xf", G + 2), ("bs", G + 2), ("bf", G), ("br", 0), ("pr", 0),
-    ("xf", G + 3), ("bs", G + 3), ("bf", G + 1), ("br", 1), ("pr", 1),
+    ("xf", G + 2), ("bs", G + 2), ("bf", G), ("br", 0), ("xf", G + 3), ("bs", G + 3), ("pr", 0),
+    ("bf", G + 1), ("br", 1), ("pr", 1),
     ("bf", G + 2), ("br", 2), ("pr", 2),
     ("bf", G + 3), ("br", 3), ("pr", 3),
 )
@@ -91,20 +93,30 @@
         first = p if which == 0 else PAIRS + 2 * p + which - 1
         return slice(first * PAIR, (first + count) * PAIR)
 
-    def weight(p, which):
+    def take(ref, sem):
+        pltpu.make_async_copy(ref, ref, sem).wait()
+
+    def part(n):
+        return slice(n * DEPTH, (n + 1) * DEPTH)
+
+    def weight(p, which, rows=slice(None), sem=None):
+        sem = load_sem.at[4 * p + which if sem is None else sem]
         cols = slice(p * PAIR, (p + 1) * PAIR)
         if which == 3:
-            return pltpu.make_async_copy(wo_h.at[cols, :], wo.at[cols, :], load_sem.at[4 * p + 3])
+            return pltpu.make_async_copy(wo_h.at[cols, :], wo.at[cols, :], sem)
         source = (wq_h, wk_h, wv_h)[which]
-        return pltpu.make_async_copy(
-            source.at[:, cols], wall.at[:, columns(p, which)], load_sem.at[4 * p + which]
-        )
-
-    load_tok = pltpu.make_async_copy(tok_h, tok, load_sem.at[4 * PAIRS])
-    load_cot = pltpu.make_async_copy(cot_h, cot, load_sem.at[4 * PAIRS + 1])
-    loads = [[load_tok, weight(0, 1), weight(0, 2)]]
-    loads += [[weight(p, 1), weight(p, 2)] for p in range(1, PAIRS)]
-    loads += [[load_cot, weight(0, 0), weight(0, 3)]]
+        return pltpu.make_async_copy(source.at[rows, cols], wall.at[rows, columns(p, which)], sem)
+
+    first = 4 * PAIRS
+    loads = []
+    for n in range(PARTS):
+        token = pltpu.make_async_copy(
+            tok_h.at[:, part(n)], tok.at[:, part(n)], load_sem.at[first + 2 * n]
+        )
+        loads += [[token, *[weight(0, which, part(n), first + 2 * n + 1) for which in (1, 2)]]]
+    loads += [[weight(p, 1, sem=4 * p + 1), weight(p, 2, sem=4 * p + 1)] for p in range(1, PAIRS)]
+    load_cot = pltpu.make_async_copy(cot_h, cot, load_sem.at[2])
+    loads += [[load_cot, weight(0, 0, sem=0), weight(0, 3)]]
     loads += [[weight(p, 0), weight(p, 3)] for p in range(1, PAIRS)]
 
     def fetch(group):
@@ -112,8 +124,15 @@
             load.start()
 
     def arrive(group):
-        for load in loads[group]:
-            load.wait()
+        if group < PARTS:
+            take(tok.at[:, part(group)], load_sem.at[first + 2 * group])
+            take(wall.at[part(group), columns(0, 1, 2)], load_sem.at[first + 2 * group + 1])
+        elif group < PARTS + PAIRS - 1:
+            p = group - PARTS + 1
+            take(wall.at[:, columns(p, 1, 2)], load_sem.at[4 * p + 1])
+        else:
+            for load in loads[group]:
+                load.wait()
 
     def remote(source, target, sent, received, device):
         return pltpu.make_async_remote_copy(
@@ -124,40 +143,31 @@
     def y_copy(m, step):
         return remote(
             sbuf.at[m, :, (y + step) % NY], ybuf.at[m, y],
-            y_send.at[m, step - 1], y_recv.at[m, step - 1], y_peer(step),
+            y_send.at[0], y_recv.at[m], y_peer(step),
         )
 
     def z_copy(m, step):
         return remote(
             zbuf.at[m, z], zbuf.at[m, z],
-            z_send.at[m, step - 1], z_recv.at[m, step - 1], z_peer(step),
+            z_send.at[0], z_recv.at[m], z_peer(step),
         )
 
     def x_copy(m, step):
         return remote(
             xown.at[m], xbuf.at[m, a],
-            x_send.at[m, step - 1], x_recv.at[m, step - 1], x_peer(step if m < GRADS else NA - step),
+            x_send.at[0], x_recv.at[m], x_peer(step if m < GRADS else NA - step),
         )
 
     def b_copy(m, step):
         return remote(
             back.at[m, (y + step) % NY], pre.at[m, :, y],
-            b_send.at[m, step - 1], b_recv.at[m, step - 1], y_peer(step),
+            b_send.at[0], b_recv.at[m], y_peer(step),
         )
 
     def start(copy, count, m):
         for step in range(1, count):
             copy(m, step).start()
 
-    def receive(copy, count, m):
-        for step in range(1, count):
-            copy(m, step).wait_recv()
-
-    def x_each(m, sending, act):
-        upward = (m < GRADS) == sending
-        for step in range(1, NA):
-            pl.when(a + step < NA if upward else a >= step)(functools.partial(act, m, step))
-
     def start_y(m):
         start(y_copy, NY, m)
 
@@ -165,13 +175,14 @@
         start(z_copy, NZ, m)
 
     def start_x(m):
-        x_each(m, True, lambda m, step: x_copy(m, step).start())
+        for step in range(1, NA):
+            pl.when(a + step < NA if m < GRADS else a >= step)(x_copy(m, step).start)
 
     def start_b(m):
         start(b_copy, NY, m)
 
     def finish_y(m):
-        receive(y_copy, NY, m)
+        take(ybuf.at[m, 1:], y_recv.at[m])
         ybuf[m, y] = sbuf[m, :, y]
         total = ybuf[m, 0].astype(F32)
         for at in range(1, NY):
@@ -179,15 +190,18 @@
         zbuf[m, z] = total.astype(BF16)
 
     def finish_z(m):
-        receive(z_copy, NZ, m)
+        take(zbuf.at[m, 1:], z_recv.at[m])
         total = zbuf[m, 0].astype(F32)
         for at in range(1, NZ):
             total = total + zbuf[m, at].astype(F32)
         xown[m] = total.astype(BF16)
 
     def finish_x(m):
-        x_each(m, False, lambda m, step: x_copy(m, step).wait_recv())
         keys = m < GRADS
+        for count in range(1, NA):
+            pl.when(a == (count if keys else NA - 1 - count))(
+                functools.partial(take, xbuf.at[m, :count], x_recv.at[m])
+            )
         total = jnp.zeros((2, ROWS, DH), F32)
         for at in range(NA):
             total = total + jnp.where(at < a if keys else at > a, xbuf[m, at].astype(F32), 0.0)
@@ -199,32 +213,39 @@
         pre[m, :, y] = back[m, y]
 
     def finish_b(m):
-        receive(b_copy, NY, m)
-
-    def states(p, kind, left, right):
+        take(pre.at[m, :, 1:], b_recv.at[m])
+
+    def states(p, kind):
+        left, right = (1, 2) if kind == 0 else (0, 3)
+        m = kind * PAIRS + p
         for head in range(2):
             cols = slice(head * DH, (head + 1) * DH)
             parts = [
-                dot(left[rows, cols], right[rows, cols], 0, 0)
+                dot(qkvg[p, left, rows, cols], qkvg[p, right, rows, cols], 0, 0)
                 for rows in (slice(0, SUB), slice(SUB, 2 * SUB))
             ]
-            m = kind * PAIRS + p
             local[m, head] = parts[kind]
             sbuf[m, head] = (parts[0] + parts[1]).astype(BF16).reshape(NY, ROWS, DH)
 
+    def keep_keys_values(p, both):
+        both = both.astype(BF16)
+        qkvg[p, 1] = both[:, :PAIR]
+        qkvg[p, 2] = both[:, PAIR:]
+
+    def first_keys_values():
+        total = 0.0
+        for n in range(PARTS):
+            arrive(n)
+            fetch(n + PARTS)
+            total = total + dot(tok[:, part(n)], wall[part(n), columns(0, 1, 2)])
+        keep_keys_values(0, total)
+
     def keys_values(p):
-        both = dot(tok[...], wall[:, columns(p, 1, 2)]).astype(BF16)
-        keys, values = both[:, :PAIR], both[:, PAIR:]
-        qkvg[p, 1] = keys
-        qkvg[p, 2] = values
-        states(p, 0, keys, values)
+        keep_keys_values(p, dot(tok[...], wall[:, columns(p, 1, 2)]))
 
     def query_grad(p):
-        query = dot(tok[...], wall[:, columns(p, 0)]).astype(BF16)
-        grad_out = dot(cot[...], wo[p * PAIR : (p + 1) * PAIR], 1, 1).astype(BF16)
-        qkvg[p, 0] = query
-        qkvg[p, 3] = grad_out
-        states(p, 1, query, grad_out)
+        qkvg[p, 0] = dot(tok[...], wall[:, columns(p, 0)]).astype(BF16)
+        qkvg[p, 3] = dot(cot[...], wo[p * PAIR : (p + 1) * PAIR], 1, 1).astype(BF16)
 
     down = lax.broadcasted_iota(jnp.int32, (SUB, SUB), 0)
     across = lax.broadcasted_iota(jnp.int32, (SUB, SUB), 1)
@@ -276,7 +297,7 @@
                 acc[n] = part
 
     blocks = {
-        "kv": keys_values, "qg": query_grad, "a": attention, "bq": between_query, "br": between_rest,
+        "kv": keys_values, "qg": query_grad, "ks": lambda p: states(p, 0), "gs": lambda p: states(p, 1), "a": attention, "bq": between_query, "br": between_rest,
         "yf": finish_y, "zf": finish_z, "xf": finish_x, "bf": finish_b,
         "ys": start_y, "zs": start_z, "xs": start_x, "bs": start_b,
         "get": fetch, "got": arrive,
@@ -284,22 +305,19 @@
         "pr": lambda p: product(columns(p, 1, 2), last=p == PAIRS - 1),
     }
 
-    fetch(0)
+    for n in range(PARTS):
+        fetch(n)
     for peer in peers:
         pl.semaphore_signal(barrier, inc=1, device_id=peer, device_id_type=MESH)
-    arrive(0)
-    fetch(1)
-    fetch(2)
-    keys_values(0)
+    first_keys_values()
     pl.semaphore_wait(barrier, len(peers))
     for name, at in ORDER:
         blocks[name](at)
 
-    for m in range(2 * PAIRS):
-        for copy, count in ((y_copy, NY), (z_copy, NZ), (b_copy, NY)):
-            for step in range(1, count):
-                copy(m, step).wait_send()
-        x_each(m, True, lambda m, step: x_copy(m, step).wait_send())
+    take(ybuf.at[:, 1:], y_send.at[0])
+    take(zbuf.at[:, 1:], z_send.at[0])
+    take(xbuf.at[:PAIRS, 1:], x_send.at[0])
+    take(back.at[:, 1:], b_send.at[0])
 
 
 def shards(tokens, cotangent, w_query, w_key, w_value, w_out):
@@ -331,15 +349,8 @@
             pltpu.VMEM((messages, NA, *slot), BF16),
             pltpu.VMEM((messages, NY, *slot), BF16),
             pltpu.VMEM((messages, 2, NY, ROWS, DH), BF16),
-            dma((4 * PAIRS + 2,)),
-            dma((messages, NY - 1)),
-            dma((messages, NY - 1)),
-            dma((messages, NZ - 1)),
-            dma((messages, NZ - 1)),
-            dma((messages, NA - 1)),
-            dma((messages, NA - 1)),
-            dma((messages, NY - 1)),
-            dma((messages, NY - 1)),
+            dma((4 * PAIRS + 2 * PARTS,)),
+            *[dma((1,)), dma((messages,))] * 4,
         ],
         compiler_params=pltpu.CompilerParams(
             collective_id=0, has_side_effects=True, vmem_limit_bytes=56 * 1024 * 1024

time: 42.3 us -> 40 us (0.946)
  Pallas kernels: 40.8 us -> 38.3 us
    pallas_call x1, Pallas kernels: 40.8 us -> 38.3 us  [shards(): pl.pallas_call(functools.partial(kernel, factor), out_shape=pltpu.VMEM((r...]
where the time goes in v4:
time: 40 us; the launch traced here: 39.7 us
  Pallas kernels  38.3 us (96%)
  local copies, waits for them, and re-layouts  1.32 us (3%)
    pallas_call x1, Pallas kernels, shards(): pl.pallas_call(functools.partial(kernel, factor), out_shape=pltpu.VMEM((r...  38.3 us
    unnamed x1, local copies, waits for them, and re-layouts  1.32 us

profile of v4, /device:TPU:0, one launch (start us, length us, event | category | flops | bytes accessed | tf_op | source)
XLA Modules:
  0.0 39.7 jit_solution(14656585132752128630)
XLA Ops:
  0.0 38.3 %shard_map.64 = bf16[512,2048]{1,0:T(8,128)(2,1)S(1)} custom-call(bf16[512,2048]{1,0:T(8,128)(2,1)} %tok_h.1, bf16[512,2048]{1,0:T(8,128)(2,1)} %cot_h.1, bf16[2048,1024]{1,0:T(8,128)(2,1)} %wq_h.1, bf16[2048,1024]{1,0:T(8,128)(2,1)} %wk_h.1, bf16[2048,1024]{1,0:T(8,128)(2,1)} %wv_h.1, bf16[1024,2048]{1,0:T(8,128)(2,1)} %wo_h.1), custom_call_target="tpu_custom_call" | custom-call | tf_op jit(solution)/shard_map/pallas_call | solution.py:330
  38.3 1.3 %copy.8 = bf16[512,2048]{1,0:T(8,128)(2,1)} copy(bf16[512,2048]{1,0:T(8,128)(2,1)S(1)} %shard_map.64) | data formatting | bytes 4194304

commit v5 on v4

--- a/solution.py
+++ b/solution.py
@@ -17,36 +17,46 @@
 PAIRS = 4
 SUB = 256
 PARTS = 4
+NX = 4
 NY = 4
 NZ = 4
-NA = 8
-ROWS = DH // NY
+NG = 2 * NY
+ROWS = DH // NG
 DEPTH = 512
 CHUNK = 512
 KEYS, GRADS = 0, PAIRS
 
 
 K, G = KEYS, GRADS
+FIRST = (4, 7, 5, 8)
 ORDER = (
     ("got", 4), ("kv", 1), ("ks", 0),
-    ("got", 5), ("get", 8), ("ys", K), ("kv", 2), ("ks", 1),
-    ("got", 6), ("get", 9), ("ys", K + 1), ("kv", 3), ("ks", 2),
-    ("got", 7), ("get", 10), ("ys", K + 2), ("qg", 0), ("ks", 3),
-    ("got", 8), ("ys", K + 3), ("yf", K), ("zs", K), ("qg", 1), ("gs", 0),
-    ("got", 9), ("ys", G), ("yf", K + 1), ("zs", K + 1), ("qg", 2), ("gs", 1),
-    ("got", 10), ("ys", G + 1), ("yf", K + 2), ("zs", K + 2), ("zf", K), ("xs", K), ("qg", 3), ("gs", 2), ("gs", 3),
-    ("ys", G + 2), ("ys", G + 3), ("yf", K + 3), ("zs", K + 3), ("zf", K + 1), ("xs", K + 1), ("yf", G), ("zs", G), ("a", 0),
-    ("zf", K + 2), ("xs", K + 2), ("yf", G + 1), ("zs", G + 1), ("a", 1),
-    ("xf", K), ("bs", K), ("zf", K + 3), ("xs", K + 3), ("a", 2),
-    ("xf", K + 1), ("bs", K + 1), ("yf", G + 2), ("zs", G + 2), ("yf", G + 3), ("zs", G + 3), ("zf", G), ("xs", G), ("a", 3),
-    ("zf", G + 1), ("xs", G + 1), ("xf", K + 2), ("bs", K + 2), ("bf", K), ("bq", 0), ("pq", 0),
-    ("xf", K + 3), ("bs", K + 3), ("zf", G + 2), ("xs", G + 2), ("bf", K + 1), ("bq", 1), ("pq", 1),
-    ("zf", G + 3), ("xs", G + 3), ("xf", G), ("bs", G), ("bf", K + 2), ("bq", 2), ("pq", 2),
-    ("xf", G + 1), ("bs", G + 1), ("bf", K + 3), ("bq", 3), ("pq", 3),
-    ("xf", G + 2), ("bs", G + 2), ("bf", G), ("br", 0), ("xf", G + 3), ("bs", G + 3), ("pr", 0),
-    ("bf", G + 1), ("br", 1), ("pr", 1),
-    ("bf", G + 2), ("br", 2), ("pr", 2),
-    ("bf", G + 3), ("br", 3), ("pr", 3),
+    ("got", 7), ("get", 6), ("ys", K), ("qg", 0), ("ks", 1),
+    ("got", 5), ("get", 9), ("ys", K + 1), ("kv", 2), ("gs", 0),
+    ("got", 8), ("get", 10), ("ys", G), ("qg", 1), ("ks", 2),
+    ("got", 6), ("ys", K + 2), ("yf", K), ("zs", K), ("kv", 3), ("gs", 1),
+    ("got", 9), ("ys", G + 1), ("yf", K + 1), ("zs", K + 1), ("qg", 2), ("ks", 3),
+    ("got", 10), ("ys", K + 3), ("yf", G), ("zs", G), ("qg", 3), ("gs", 2), ("gs", 3),
+    ("ys", G + 2), ("ys", G + 3), ("zf", K), ("xs", K), ("zf", K + 1), ("xs", K + 1), ("yf", K + 2), ("zs", K + 2), ("yf", G + 1), ("zs", G + 1), ("a", 0),
+    ("zf", G), ("xs", G), ("a", 1),
+    ("xf", K), ("bs", K), ("yf", K + 3), ("zs", K + 3), ("a", 2),
+    ("xf", K + 1), ("bs", K + 1), ("zf", K + 2), ("xs", K + 2), ("zf", G + 1), ("xs", G + 1), ("yf", G + 2), ("zs", G + 2), ("yf", G + 3), ("zs", G + 3), ("a", 3),
+    ("xf", G), ("bs", G), ("zf", K + 3), ("xs", K + 3), ("bf", K), ("bq", 0),
+    ("xf", K + 2), ("bs", K + 2), ("xf", G + 1), ("bs", G + 1), ("pq", 0),
+    ("zf", G + 2), ("xs", G + 2), ("bf", K + 1), ("bq", 1),
+    ("pq", 1),
+    ("zf", G + 3), ("xs", G + 3), ("bf", G), ("br", 0),
+    ("xf", K + 3), ("bs", K + 3), ("pr", 0),
+    ("xf", G + 2), ("bs", G + 2), ("bf", K + 2), ("bq", 2),
+    ("pq", 2),
+    ("bf", G + 1), ("br", 1),
+    ("xf", G + 3), ("bs", G + 3), ("pr", 1),
+    ("bf", K + 3), ("bq", 3),
+    ("pq", 3),
+    ("bf", G + 2), ("br", 2),
+    ("pr", 2),
+    ("bf", G + 3), ("br", 3),
+    ("pr", 3),
 )
 
 
@@ -73,21 +83,24 @@
 ):
     a = lax.axis_index("ctxa")
     b = lax.axis_index("ctxb")
+    x, core = a // 2, a % 2
     z, y = b // NY, b % NY
-
-    def y_peer(step):
-        return (a, z * NY + (y + step) % NY)
+    g = core * NY + y
+
+    def g_peer(step):
+        at = (g + step) % NG
+        return (2 * x + at // NY, z * NY + at % NY)
 
     def z_peer(step):
         return (a, ((z + step) % NZ) * NY + y)
 
     def x_peer(step):
-        return ((a + step) % NA, b)
+        return (2 * ((x + step) % NX) + core, b)
 
     barrier = pltpu.get_barrier_semaphore()
-    peers = [y_peer(s) for s in range(1, NY)]
+    peers = [g_peer(s) for s in range(1, NG)]
     peers += [z_peer(s) for s in range(1, NZ)]
-    peers += [x_peer(s) for s in range(1, NA)]
+    peers += [x_peer(s) for s in range(1, NX)]
 
     def columns(p, which, count=1):
         first = p if which == 0 else PAIRS + 2 * p + which - 1
@@ -142,8 +155,8 @@
 
     def y_copy(m, step):
         return remote(
-            sbuf.at[m, :, (y + step) % NY], ybuf.at[m, y],
-            y_send.at[0], y_recv.at[m], y_peer(step),
+            sbuf.at[m, :, (g + step) % NG], ybuf.at[m, g],
+            y_send.at[0], y_recv.at[m], g_peer(step),
         )
 
     def z_copy(m, step):
@@ -154,14 +167,14 @@
 
     def x_copy(m, step):
         return remote(
-            xown.at[m], xbuf.at[m, a],
-            x_send.at[0], x_recv.at[m], x_peer(step if m < GRADS else NA - step),
+            xown.at[m], xbuf.at[m, x],
+            x_send.at[0], x_recv.at[m], x_peer(step if m < GRADS else NX - step),
         )
 
     def b_copy(m, step):
         return remote(
-            back.at[m, (y + step) % NY], pre.at[m, :, y],
-            b_send.at[0], b_recv.at[m], y_peer(step),
+            back.at[m, (g + step) % NG], pre.at[m, :, g],
+            b_send.at[0], b_recv.at[m], g_peer(step),
         )
 
     def start(copy, count, m):
@@ -169,48 +182,53 @@
             copy(m, step).start()
 
     def start_y(m):
-        start(y_copy, NY, m)
+        start(y_copy, NG, m)
 
     def start_z(m):
         start(z_copy, NZ, m)
 
     def start_x(m):
-        for step in range(1, NA):
-            pl.when(a + step < NA if m < GRADS else a >= step)(x_copy(m, step).start)
+        for step in range(1, NX):
+            pl.when(x + step < NX if m < GRADS else x >= step)(x_copy(m, step).start)
 
     def start_b(m):
-        start(b_copy, NY, m)
+        start(b_copy, NG, m)
+
+    def sum_of(parts):
+        return functools.reduce(lambda total, part: total + part, parts)
 
     def finish_y(m):
         take(ybuf.at[m, 1:], y_recv.at[m])
-        ybuf[m, y] = sbuf[m, :, y]
-        total = ybuf[m, 0].astype(F32)
-        for at in range(1, NY):
-            total = total + ybuf[m, at].astype(F32)
-        zbuf[m, z] = total.astype(BF16)
+        ybuf[m, g] = sbuf[m, :, g]
+        for half in range(2):
+            line = range(half * NY, (half + 1) * NY)
+            zbuf[m, z, half] = sum_of(ybuf[m, at].astype(F32) for at in line).astype(BF16)
 
     def finish_z(m):
         take(zbuf.at[m, 1:], z_recv.at[m])
-        total = zbuf[m, 0].astype(F32)
-        for at in range(1, NZ):
-            total = total + zbuf[m, at].astype(F32)
-        xown[m] = total.astype(BF16)
+        both = sum_of(zbuf[m, at].astype(F32) for at in range(NZ))
+        xown[m] = (both[0] + both[1]).astype(BF16)
 
     def finish_x(m):
         keys = m < GRADS
-        for count in range(1, NA):
-            pl.when(a == (count if keys else NA - 1 - count))(
+        for count in range(1, NX):
+            pl.when(x == (count if keys else NX - 1 - count))(
                 functools.partial(take, xbuf.at[m, :count], x_recv.at[m])
             )
-        total = jnp.zeros((2, ROWS, DH), F32)
-        for at in range(NA):
-            total = total + jnp.where(at < a if keys else at > a, xbuf[m, at].astype(F32), 0.0)
-        for at in range(NZ):
-            total = total + jnp.where(at < z if keys else at > z, zbuf[m, at].astype(F32), 0.0)
-        for at in range(NY) if keys else reversed(range(NY)):
-            back[m, at] = total.astype(BF16)
-            total = total + ybuf[m, at].astype(F32)
-        pre[m, :, y] = back[m, y]
+        outer = sum_of(
+            jnp.where(at < x if keys else at > x, xbuf[m, at].astype(F32), 0.0) for at in range(NX)
+        )
+        for half in (0, 1) if keys else (1, 0):
+            planes = [zbuf[m, at, half].astype(F32) for at in range(NZ)]
+            total = outer + sum_of(
+                jnp.where(at < z if keys else at > z, planes[at], 0.0) for at in range(NZ)
+            )
+            outer = outer + sum_of(planes)
+            line = range(half * NY, (half + 1) * NY)
+            for at in line if keys else reversed(line):
+                back[m, at] = total.astype(BF16)
+                total = total + ybuf[m, at].astype(F32)
+        pre[m, :, g] = back[m, g]
 
     def finish_b(m):
         take(pre.at[m, :, 1:], b_recv.at[m])
@@ -225,7 +243,7 @@
                 for rows in (slice(0, SUB), slice(SUB, 2 * SUB))
             ]
             local[m, head] = parts[kind]
-            sbuf[m, head] = (parts[0] + parts[1]).astype(BF16).reshape(NY, ROWS, DH)
+            sbuf[m, head] = (parts[0] + parts[1]).astype(BF16).reshape(NG, ROWS, DH)
 
     def keep_keys_values(p, both):
         both = both.astype(BF16)
@@ -236,7 +254,7 @@
         total = 0.0
         for n in range(PARTS):
             arrive(n)
-            fetch(n + PARTS)
+            fetch(FIRST[n])
             total = total + dot(tok[:, part(n)], wall[part(n), columns(0, 1, 2)])
         keep_keys_values(0, total)
 
@@ -342,13 +360,13 @@
             pltpu.VMEM((rows, 3 * PAIRS * PAIR), BF16),
             pltpu.VMEM((width // CHUNK, rows, CHUNK), F32),
             pltpu.VMEM((messages, 2, DH, DH), F32),
-            pltpu.VMEM((messages, 2, NY, ROWS, DH), BF16),
-            pltpu.VMEM((messages, NY, *slot), BF16),
-            pltpu.VMEM((messages, NZ, *slot), BF16),
+            pltpu.VMEM((messages, 2, NG, ROWS, DH), BF16),
+            pltpu.VMEM((messages, NG, *slot), BF16),
+            pltpu.VMEM((messages, NZ, 2, *slot), BF16),
             pltpu.VMEM((messages, *slot), BF16),
-            pltpu.VMEM((messages, NA, *slot), BF16),
-            pltpu.VMEM((messages, NY, *slot), BF16),
-            pltpu.VMEM((messages, 2, NY, ROWS, DH), BF16),
+            pltpu.VMEM((messages, NX, *slot), BF16),
+            pltpu.VMEM((messages, NG, *slot), BF16),
+            pltpu.VMEM((messages, 2, NG, ROWS, DH), BF16),
             dma((4 * PAIRS + 2 * PARTS,)),
             *[dma((1,)), dma((messages,))] * 4,
         ],

time: 40 us -> 39 us (0.975)
  Pallas kernels: 38.3 us -> 37 us
    pallas_call x1, Pallas kernels: 38.3 us -> 37 us  [shards(): pl.pallas_call(functools.partial(kernel, factor), out_shape=pltpu.VMEM((r...]
where the time goes in v5:
time: 39 us; the launch traced here: 38.4 us
  Pallas kernels  37 us (95%)
  local copies, waits for them, and re-layouts  1.32 us (3%)
    pallas_call x1, Pallas kernels, shards(): pl.pallas_call(functools.partial(kernel, factor), out_shape=pltpu.VMEM((r...  37 us
    unnamed x1, local copies, waits for them, and re-layouts  1.32 us

profile of v5, /device:TPU:0, one launch (start us, length us, event | category | flops | bytes accessed | tf_op | source)
XLA Modules:
  0.0 38.4 jit_solution(6280189497799539814)
XLA Ops:
  0.0 37.0 %shard_map.64 = bf16[512,2048]{1,0:T(8,128)(2,1)S(1)} custom-call(bf16[512,2048]{1,0:T(8,128)(2,1)} %tok_h.1, bf16[512,2048]{1,0:T(8,128)(2,1)} %cot_h.1, bf16[2048,1024]{1,0:T(8,128)(2,1)} %wq_h.1, bf16[2048,1024]{1,0:T(8,128)(2,1)} %wk_h.1, bf16[2048,1024]{1,0:T(8,128)(2,1)} %wv_h.1, bf16[1024,2048]{1,0:T(8,128)(2,1)} %wo_h.1), custom_call_target="tpu_custom_call" | custom-call | tf_op jit(solution)/shard_map/pallas_call | solution.py:348
  37.1 1.3 %copy.8 = bf16[512,2048]{1,0:T(8,128)(2,1)} copy(bf16[512,2048]{1,0:T(8,128)(2,1)S(1)} %shard_map.64) | data formatting | bytes 4194304

commit v6 on v5

--- a/solution.py
+++ b/solution.py
@@ -56,7 +56,6 @@
     ("bf", G + 2), ("br", 2),
     ("pr", 2),
     ("bf", G + 3), ("br", 3),
-    ("pr", 3),
 )
 
 
@@ -75,8 +74,8 @@
 
 def kernel(
     factor,
-    tok_h, cot_h, wq_h, wk_h, wv_h, wo_h, out,
-    tok, cot, wall, wo, qkvg, intra, grads, acc,
+    tok_h, cot_h, wq_h, wk_h, wv_h, wo_h, acc, grads, wall,
+    tok, cot, wo, qkvg, intra,
     local, sbuf, ybuf, zbuf, xown, xbuf, back, pre,
     load_sem,
     y_send, y_recv, z_send, z_recv, x_send, x_recv, b_send, b_recv,
@@ -304,15 +303,11 @@
             finish(p, 1, rows, dot(qkvg[p, 2, rows], after, 1, 1))
             finish(p, 2, rows, dot(qkvg[p, 1, rows], after, 1, 0))
 
-    def product(cols, first=False, last=False):
+    def product(cols, first=False):
         for n in range(acc.shape[0]):
             rows = slice(n * CHUNK, (n + 1) * CHUNK)
             part = dot(grads[:, cols], wall[rows, cols], 1, 1)
-            part = part if first else acc[n] + part
-            if last:
-                out[:, rows] = part.astype(BF16)
-            else:
-                acc[n] = part
+            acc[n] = part if first else acc[n] + part
 
     blocks = {
         "kv": keys_values, "qg": query_grad, "ks": lambda p: states(p, 0), "gs": lambda p: states(p, 1), "a": attention, "bq": between_query, "br": between_rest,
@@ -320,7 +315,7 @@
         "ys": start_y, "zs": start_z, "xs": start_x, "bs": start_b,
         "get": fetch, "got": arrive,
         "pq": lambda p: product(columns(p, 0), first=p == 0),
-        "pr": lambda p: product(columns(p, 1, 2), last=p == PAIRS - 1),
+        "pr": lambda p: product(columns(p, 1, 2)),
     }
 
     for n in range(PARTS):
@@ -338,6 +333,18 @@
     take(back.at[:, 1:], b_send.at[0])
 
 
+def last_kernel(acc, grads, wall, out_h, outs, sem):
+    cols = slice((3 * PAIRS - 2) * PAIR, 3 * PAIRS * PAIR)
+    copies = []
+    for n in range(acc.shape[0]):
+        rows = slice(n * CHUNK, (n + 1) * CHUNK)
+        outs[n] = (acc[n] + dot(grads[:, cols], wall[rows, cols], 1, 1)).astype(BF16)
+        copies.append(pltpu.make_async_copy(outs.at[n], out_h.at[:, rows], sem.at[n]))
+        copies[n].start()
+    for copy in copies:
+        copy.wait()
+
+
 def shards(tokens, cotangent, w_query, w_key, w_value, w_out):
     rows, width = tokens.shape
     blocks = lax.axis_size("ctxa") * lax.axis_size("ctxb")
@@ -345,20 +352,22 @@
     slot = (2, ROWS, DH)
     messages = 2 * PAIRS
     dma = pltpu.SemaphoreType.DMA
-    return pl.pallas_call(
+    steps = width // CHUNK
+    parts = pl.pallas_call(
         functools.partial(kernel, factor),
-        out_shape=pltpu.VMEM((rows, width), BF16),
+        out_shape=[
+            pltpu.VMEM((steps, rows, CHUNK), F32),
+            pltpu.VMEM((rows, 3 * PAIRS * PAIR), BF16),
+            pltpu.VMEM((width, 3 * PAIRS * PAIR), BF16),
+        ],
         in_specs=[pl.BlockSpec(memory_space=pl.ANY)] * 6,
-        out_specs=pl.BlockSpec(memory_space=pltpu.VMEM),
+        out_specs=[pl.BlockSpec(memory_space=pltpu.VMEM)] * 3,
         scratch_shapes=[
             pltpu.VMEM((rows, width), BF16),
             pltpu.VMEM((rows, width), BF16),
-            pltpu.VMEM((width, 3 * PAIRS * PAIR), BF16),
             pltpu.VMEM((PAIRS * PAIR, width), BF16),
             pltpu.VMEM((PAIRS, 4, rows, PAIR), BF16),
             pltpu.VMEM((PAIRS, 3, rows, PAIR), F32),
-            pltpu.VMEM((rows, 3 * PAIRS * PAIR), BF16),
-            pltpu.VMEM((width // CHUNK, rows, CHUNK), F32),
             pltpu.VMEM((messages, 2, DH, DH), F32),
             pltpu.VMEM((messages, 2, NG, ROWS, DH), BF16),
             pltpu.VMEM((messages, NG, *slot), BF16),
@@ -371,9 +380,17 @@
             *[dma((1,)), dma((messages,))] * 4,
         ],
         compiler_params=pltpu.CompilerParams(
-            collective_id=0, has_side_effects=True, vmem_limit_bytes=56 * 1024 * 1024
+            collective_id=0, has_side_effects=True, vmem_limit_bytes=40 * 1024 * 1024
         ),
     )(tokens, cotangent, w_query, w_key, w_value, w_out)
+    return pl.pallas_call(
+        last_kernel,
+        out_shape=jax.ShapeDtypeStruct((rows, width), BF16),
+        in_specs=[pl.BlockSpec(memory_space=pltpu.VMEM)] * 3,
+        out_specs=pl.BlockSpec(memory_space=pl.ANY),
+        scratch_shapes=[pltpu.VMEM((steps, rows, CHUNK), BF16), dma((steps,))],
+        compiler_params=pltpu.CompilerParams(vmem_limit_bytes=16 * 1024 * 1024),
+    )(*parts)
 
 
 def solution(mesh):

time: 39 us -> 38.9 us (level)
  local copies, waits for them, and re-layouts: 1.32 us -> 0 us
  Pallas kernels: 37 us -> 38.1 us
    unnamed x1 -> x0, local copies, waits for them, and re-layouts: 1.32 us -> none
    pallas_call x1 -> x2, Pallas kernels: 37 us -> 38.1 us  [the longest x1 36 us: shards(): pl.pallas_call(functools.partial(kernel, factor), out_shape=[pltpu.VMEM((...]
where the time goes in v6:
time: 38.9 us; the launch traced here: 38.3 us
  Pallas kernels  38.1 us (98%)
    pallas_call x1, Pallas kernels, shards(): pl.pallas_call(functools.partial(kernel, factor), out_shape=[pltpu.VMEM((...  36 us
    pallas_call x1, Pallas kernels, shards(): pl.pallas_call(last_kernel, out_shape=jax.ShapeDtypeStruct((rows, width),...  2.12 us

profile of v6, /device:TPU:0, one launch (start us, length us, event | category | flops | bytes accessed | tf_op | source)
XLA Modules:
  0.0 38.3 jit_solution(12712451389904342068)
XLA Ops:
  0.0 36.0 %shard_map.64 = (f32[4,512,512]{2,1,0:T(8,128)S(1)}, bf16[512,3072]{1,0:T(8,128)(2,1)S(1)}, bf16[2048,3072]{1,0:T(8,128)(2,1)S(1)}) custom-call(bf16[512,2048]{1,0:T(8,128)(2,1)} %tok_h.1, bf16[512,2048]{1,0:T(8,128)(2,1)} %cot_h.1, bf16[2048,1024]{1,0:T(8,128)(2,1)} %wq_h.1, bf16[2048,1024]{1,0:T(8,128)(2,1)} %wk_h.1, bf16[2048,1024]{1,0:T(8,128)(2,1)} %wv_h.1, ...), custom_call_target="tpu_custom_call" | custom-call | tf_op jit(solution)/shard_map/pallas_call | solution.py:356
  36.0 2.1 %shard_map.65 = bf16[512,2048]{1,0:T(8,128)(2,1)} custom-call(f32[4,512,512]{2,1,0:T(8,128)S(1)} %get-tuple-element.8.acc, bf16[512,3072]{1,0:T(8,128)(2,1)S(1)} %get-tuple-element.9.grads, bf16[2048,3072]{1,0:T(8,128)(2,1)S(1)} %get-tuple-element.10.wall), custom_call_target="tpu_custom_call" | custom-call | tf_op jit(solution)/shard_map/pallas_call | solution.py:386
